TPU v7x, 256 devices: a whole 4x4x8 slice. The times are simulated.
256 devices in a mesh: dp: 8 (over x, core), graph: 32 (over y, z).
Axes of the slice: x: 4, y: 4, z: 8, core: 2. Of those that a mesh axis runs over, the one named last changes fastest.
Arguments:
- edges: bfloat16 [8, 65536, 1024], P('dp', 'graph'), may hold values from -6 to 6
- send_rows: int32 [8, 262144], P('dp', 'graph'), may hold values from 0 to 2047
- trip_src: int32 [8, 262144], P('dp', 'graph'), may hold values from 0 to 8191
- trip_dst: int32 [8, 262144], P('dp', 'graph'), may hold values from 0 to 2047
- basis_values: bfloat16 [8, 42, 262144], P('dp', None, 'graph'), may hold values from -6 to 6
- cotangent: bfloat16 [8, 65536, 1024], P('dp', 'graph'), may hold values from -6 to 6
- w_down: bfloat16 [1024, 128], replicated, may hold values from -0.1875 to 0.1875
- w_up: bfloat16 [128, 1024], replicated, may hold values from -0.5 to 0.5
- w_basis: bfloat16 [42, 128], replicated, may hold values from -1 to 1
Outputs:
- grad_edges: bfloat16 [8, 65536, 1024], P('dp', 'graph')
- grad_down: float32 [1024, 128], replicated
- grad_up: float32 [128, 1024], replicated
- grad_basis: float32 [42, 128], replicated
All inputs are finite; a program needn't handle non-finite values.
Results may differ from a plain program's by a relative error of at most 0.0073.
Values may be sent and summed in bfloat16 or wider, within the bound.
No kernel may reach another device: no remote copies, remote signals or barrier semaphores. Data moves between devices by JAX's collectives and lax.ppermute only.
A program may use at most 128 MiB of HBM per device.

v0:
```python
import jax
import jax.numpy as jnp
from jax import lax
from jax.sharding import PartitionSpec as P


def shards(edges, send_rows, trip_src, trip_dst, basis_values, cotangent, w_down, w_up, w_basis):
    edge_rows = edges[0]
    sendlist = send_rows[0]
    source_index = trip_src[0]
    target_index = trip_dst[0]
    basis_block = basis_values[0]
    grad_block = cotangent[0]
    local_edges = edge_rows.shape[0]
    down = jnp.dot(edge_rows, w_down, preferred_element_type=jnp.float32).astype(jnp.bfloat16)
    received = lax.all_to_all(
        jnp.take(down, sendlist, axis=0), "graph", split_axis=0, concat_axis=0, tiled=True
    )
    asked_rows = received.shape[0]
    source_rows = jnp.take(received, source_index, axis=0).astype(jnp.float32)
    basis_emb = lax.dot_general(
        basis_block, w_basis, (((0,), (0,)), ((), ())), preferred_element_type=jnp.float32
    )
    product = source_rows * basis_emb
    aggregate = jax.ops.segment_sum(product, target_index, num_segments=local_edges).astype(
        jnp.bfloat16
    )
    pre_act = jnp.dot(aggregate, w_up, preferred_element_type=jnp.float32)
    sigma = jax.nn.sigmoid(pre_act)
    g_pre = (grad_block.astype(jnp.float32) * sigma * (1.0 + pre_act * (1.0 - sigma))).astype(
        jnp.bfloat16
    )
    up_term = lax.dot_general(
        aggregate, g_pre, (((0,), (0,)), ((), ())), preferred_element_type=jnp.float32
    )
    g_agg = lax.dot_general(
        g_pre, w_up, (((1,), (1,)), ((), ())), preferred_element_type=jnp.float32
    )
    g_trip = jnp.take(g_agg, target_index, axis=0)
    g_source = g_trip * basis_emb
    g_basis_emb = g_trip * source_rows
    basis_term = jnp.dot(
        basis_block.astype(jnp.float32), g_basis_emb, precision=lax.Precision.HIGHEST
    )
    g_received = jax.ops.segment_sum(g_source, source_index, num_segments=asked_rows)
    returned = lax.all_to_all(g_received, "graph", split_axis=0, concat_axis=0, tiled=True)
    g_down = jax.ops.segment_sum(returned, sendlist, num_segments=local_edges).astype(jnp.bfloat16)
    grad_edges = lax.dot_general(
        g_down, w_down, (((1,), (1,)), ((), ())), preferred_element_type=jnp.float32
    )
    down_term = lax.dot_general(
        edge_rows, g_down, (((0,), (0,)), ((), ())), preferred_element_type=jnp.float32
    )
    grad_down, grad_up, grad_basis = lax.psum((down_term, up_term, basis_term), ("dp", "graph"))
    return (grad_edges.astype(jnp.bfloat16)[None], grad_down, grad_up, grad_basis)


def solution(mesh):
    in_specs = (
        P("dp", "graph", None),
        P("dp", "graph"),
        P("dp", "graph"),
        P("dp", "graph"),
        P("dp", None, "graph"),
        P("dp", "graph", None),
        P(),
        P(),
        P(),
    )
    out_specs = (P("dp", "graph", None), P(), P(), P())
    return jax.shard_map(shards, mesh=mesh, in_specs=in_specs, out_specs=out_specs, check_vma=False)
```

profile of v0, /device:TPU:1, one launch (start us, length us, event | category | flops | bytes accessed | tf_op | source)
XLA Modules:
  0.0 684.8 jit_solution(6888944162113069686)
XLA Ops:
  8.6 1.5 reduce.3
  10.1 3.5 fusion.12
  13.6 24.0 %gather_fusion = bf16[8192,128]{1,0:T(8,128)(2,1)S(1)} fusion(bf16[2048,128]{1,0:T(8,128)(2,1)S(1)} %fusion.12, s32[8192]{0:T(1024)S(1)} %broadcast_clamp_fusion.2), kind=kCustom, calls=%fused_computation | custom fusion | bytes 4227072 | tf_op jit(solution)/shard_map/jit(_take)/gather | solution.py:17
  37.7 2.7 broadcast_select_fusion.1
  40.3 12.0 %all-to-all-start = ((bf16[32,256,128]{2,1,0:T(8,128)(2,1)}), bf16[32,256,128]{2,1,0:T(8,128)(2,1)S(1)}, u32[]{:S(2)}, u32[]{:S(2)}) async-start(bf16[32,256,128]{2,1,0:T(8,128)(2,1)} %broadcast_select_fusion.1), calls=%async_computation | async-start | bytes 4194304 | tf_op jit(solution)/shard_map/all_to_all | solution.py:16
  52.5 2.8 fusion.25
  55.3 45.9 %all-to-all-done = bf16[32,256,128]{2,1,0:T(8,128)(2,1)S(1)} async-done(((bf16[32,256,128]{2,1,0:T(8,128)(2,1)}), bf16[32,256,128]{2,1,0:T(8,128)(2,1)S(1)}, u32[]{:S(2)}, u32[]{:S(2)}) %all-to-all-start) | async-done | bytes 2097184 | tf_op jit(solution)/shard_map/all_to_all | solution.py:16
  101.2 29.4 %gather_fusion.1 = bf16[8192,128]{1,0:T(8,128)(2,1)} fusion(bf16[8192,128]{1,0:T(8,128)(2,1)S(1)} %bitcast.46, s32[8192]{0:T(1024)S(1)} %broadcast_clamp_fusion), kind=kCustom, calls=%fused_computation.1 | custom fusion | bytes 4227072 | tf_op jit(solution)/shard_map/jit(_take)/gather | solution.py:20
  130.6 49.5 %scatter_custom_fusion = f32[2048,128]{1,0:T(8,128)S(1)} fusion(s32[8192]{0:T(1024)S(1)} %bitcast.50, f32[8192,128]{1,0:T(8,128)} %fusion.25, bf16[8192,128]{1,0:T(8,128)(2,1)} %gather_fusion.1, pred[8192]{0:T(1024)(128)(4,1)S(1)} %get-tuple-element.14, bf16[]{:T(256)} %constant.46.clone.1, f32[]{:T(128)} %constant.30.clone.1), kind=kCustom, calls=%fused_computation.11 | custom fusion | flops 4194304 | bytes 7348230 | tf_op jit(solution)/shard_map/scatter-add | solution.py:25
  180.2 5.7 fusion.1
  185.8 2.0 copy-done.1
  189.1 27.8 %gather_fusion.2 = f32[8192,128]{1,0:T(8,128)} fusion(f32[2048,128]{1,0:T(8,128)S(1)} %fusion.37, s32[8192]{0:T(1024)S(1)} %broadcast_clamp_fusion.1), kind=kCustom, calls=%fused_computation.2 | custom fusion | bytes 8421376 | tf_op jit(solution)/shard_map/jit(_take)/gather | solution.py:39
  216.9 51.4 %scatter_custom_fusion.1 = f32[8192,128]{1,0:T(8,128)} fusion(s32[8192]{0:T(1024)S(1)} %bitcast.52, f32[8192,128]{1,0:T(8,128)} %fusion.25, f32[8192,128]{1,0:T(8,128)} %gather_fusion.2, f32[]{:T(128)} %constant.47.clone.1, f32[]{:T(128)} %constant.30.clone.1, pred[8192]{0:T(1024)(128)(4,1)S(1)} %get-tuple-element.15), kind=kCustom, calls=%fused_computation.18 | custom fusion | flops 3145728 | bytes 12591112 | tf_op jit(solution)/shard_map/scatter-add | solution.py:45
  268.3 7.2 %all-to-all-start.1 = ((f32[32,256,128]{2,1,0:T(8,128)}), f32[32,256,128]{2,1,0:T(8,128)}, u32[]{:S(2)}, u32[]{:S(2)}) async-start(f32[32,256,128]{2,1,0:T(8,128)} %bitcast.47), calls=%async_computation.1 | async-start | bytes 8388608 | tf_op jit(solution)/shard_map/all_to_all | solution.py:46
  275.6 3.7 fusion.32
  279.3 88.9 %all-to-all-done.1 = f32[32,256,128]{2,1,0:T(8,128)} async-done(((f32[32,256,128]{2,1,0:T(8,128)}), f32[32,256,128]{2,1,0:T(8,128)}, u32[]{:S(2)}, u32[]{:S(2)}) %all-to-all-start.1) | async-done | bytes 4194336 | tf_op jit(solution)/shard_map/all_to_all | solution.py:46
  368.2 45.4 %scatter_custom_fusion.2 = f32[2048,128]{1,0:T(8,128)} fusion(s32[8192]{0:T(1024)} %bitcast.53, f32[8192,128]{1,0:T(8,128)} %bitcast.15, f32[]{:T(128)} %constant.30.clone.1), kind=kCustom, calls=%fused_computation.35 | custom fusion | flops 1048576 | bytes 1049088 | tf_op jit(solution)/shard_map/scatter-add | solution.py:47
  413.6 4.1 fusion.20
  417.7 7.1 %fusion.23 = f32[42,128]{1,0:T(8,128)S(1)} fusion(f32[8192,128]{1,0:T(8,128)} %gather_fusion.2, pred[8192]{0:T(1024)(128)(4,1)S(1)} %get-tuple-element.15, bf16[8192,128]{1,0:T(8,128)(2,1)S(1)} %copy-done.2, pred[8192]{0:T(1024)(128)(4,1)S(1)} %get-tuple-element.14, bf16[1,42,8192]{2,1,0:T(8,128)(2,1)S(1)} %copy-done), kind=kOutput, calls=%fused_computation.31 | convolution fusion | flops 532676608 | bytes 7017472 | tf_op jit(solution)/shard_map/dot_general | solution.py:42
  424.7 79.8 %psum.23 = f32[42,128]{1,0:T(8,128)} all-reduce(f32[42,128]{1,0:T(8,128)S(1)} %fusion.23), channel_id=1, replica_groups=mesh['dp'=8,'graph'=32] {'dp','graph'}, use_global_device_ids=true, to_apply=%region_5.6 | all-reduce | flops 5376 | bytes 43008 | tf_op jit(solution)/shard_map/psum | solution.py:54
  504.5 4.5 convert_bitcast_fusion
  509.0 165.0 %all-reduce.3.cloned.1.call-done = (f32[1024,128]{0,1:T(8,128)}, f32[128,1024]{1,0:T(8,128)}) async-done(((f32[1024,128]{0,1:T(8,128)}, f32[128,1024]{1,0:T(8,128)}), (f32[1024,128]{0,1:T(8,128)}, f32[128,1024]{1,0:T(8,128)})) %all-reduce.3.cloned.1.call-update) | async-done | bytes 1048592 | tf_op jit(solution)/shard_map/psum | solution.py:54
  674.0 2.0 copy.14
  676.1 1.9 copy.17
  (28 shorter events, 2.9 us)
Async XLA Ops:
  7.2 45.4 %copy-start = (bf16[1,42,8192]{2,1,0:T(8,128)(2,1)S(1)}, bf16[1,42,8192]{2,1,0:T(8,128)(2,1)}, u32[]{:S(2)}) copy-start(bf16[1,42,8192]{2,1,0:T(8,128)(2,1)} %param.13) | copy-start | bytes 2064388
  37.6 14.7 %copy-start.6 = (s32[1,8192]{1,0:T(1,128)S(1)}, s32[1,8192]{1,0:T(1,128)}, u32[]{:S(2)}) copy-start(s32[1,8192]{1,0:T(1,128)} %param.11) | copy-start | bytes 98308
  37.6 14.8 %copy-start.5 = (s32[1,8192]{1,0:T(1,128)S(1)}, s32[1,8192]{1,0:T(1,128)}, u32[]{:S(2)}) copy-start(s32[1,8192]{1,0:T(1,128)} %param.12) | copy-start | bytes 98308
  37.6 14.9 %copy-start.7 = (bf16[42,128]{1,0:T(8,128)(2,1)S(1)}, bf16[42,128]{1,0:T(8,128)(2,1)}, u32[]{:S(2)}) copy-start(bf16[42,128]{1,0:T(8,128)(2,1)} %param.17) | copy-start | bytes 32260
  40.3 60.9 %all-to-all-start = ((bf16[32,256,128]{2,1,0:T(8,128)(2,1)}), bf16[32,256,128]{2,1,0:T(8,128)(2,1)S(1)}, u32[]{:S(2)}, u32[]{:S(2)}) async-start(bf16[32,256,128]{2,1,0:T(8,128)(2,1)} %broadcast_select_fusion.1), calls=%async_computation | async-start | bytes 4194304 | tf_op jit(solution)/shard_map/all_to_all | solution.py:16
  130.6 49.5 %copy-start.3 = (bf16[128,1024]{1,0:T(8,128)(2,1)S(1)}, bf16[128,1024]{1,0:T(8,128)(2,1)}, u32[]{:S(2)}) copy-start(bf16[128,1024]{1,0:T(8,128)(2,1)} %param.16) | copy-start | bytes 786436
  185.8 2.0 copy-start.1
  268.3 99.8 %all-to-all-start.1 = ((f32[32,256,128]{2,1,0:T(8,128)}), f32[32,256,128]{2,1,0:T(8,128)}, u32[]{:S(2)}, u32[]{:S(2)}) async-start(f32[32,256,128]{2,1,0:T(8,128)} %bitcast.47), calls=%async_computation.1 | async-start | bytes 8388608 | tf_op jit(solution)/shard_map/all_to_all | solution.py:46
  275.5 398.5 %all-reduce.3.cloned.1.call-start = ((), (), s32[]{:S(2)}) async-start(), calls=%async_computation.2 | async-start | bytes 2097152 | tf_op jit(solution)/shard_map/psum | solution.py:54
  279.3 138.4 %copy-start.2 = (bf16[8192,128]{1,0:T(8,128)(2,1)S(1)}, bf16[8192,128]{1,0:T(8,128)(2,1)}, u32[]{:S(2)}) copy-start(bf16[8192,128]{1,0:T(8,128)(2,1)} %gather_fusion.1) | copy-start | bytes 6291460
  417.6 86.9 %copy-start.4 = (bf16[1024,128]{1,0:T(8,128)(2,1)S(1)}, bf16[1024,128]{1,0:T(8,128)(2,1)}, u32[]{:S(2)}) copy-start(bf16[1024,128]{1,0:T(8,128)(2,1)} %param.15) | copy-start | bytes 786436
Sparse Core Ops, SparseCore 0:
  417.8 256.2 all-reduce.2
where the time goes:
time: 686 us; the launch traced here: 685 us
  waiting for transfers between devices  300 us (44%)
  other arithmetic  151 us (22%)
  local copies, waits for them, and re-layouts  87.8 us (13%)
  blocking collectives  79.8 us (12%)
  matrix products  32.5 us (5%)
  starting transfers between devices  19.2 us (3%)
  between operations  14.3 us (2%)
    psum x1, waiting for transfers between devices, shards(): lax.psum((down_term, up_term, basis_term), ('dp', 'graph'))  165 us
    all_to_all x1, waiting for transfers between devices, shards(): lax.all_to_all(g_received, 'graph', split_axis=0, concat_axis=0, tiled=True)  88.9 us
    psum x1, blocking collectives, shards(): lax.psum((down_term, up_term, basis_term), ('dp', 'graph'))  79.8 us
    scatter-add x1, other arithmetic, shards(): jax.ops.segment_sum(g_source, source_index, num_segments=asked_rows)  51.4 us
    scatter-add x1, other arithmetic, shards(): jax.ops.segment_sum(product, target_index, num_segments=local_edges)  49.5 us
    all_to_all x1, waiting for transfers between devices, shards(): lax.all_to_all(jnp.take(down, sendlist, axis=0), 'graph', split_axis=0, c...  45.9 us
    scatter-add x1, other arithmetic, shards(): jax.ops.segment_sum(returned, sendlist, num_segments=local_edges)  45.4 us
    gather x1, local copies, waits for them, and re-layouts, shards(): source_rows = jnp.take(received, source_index, axis=0).astype(jnp.float32)  29.4 us
  transfers between devices with their start and end apart: 3, of which 3 were waited for; matrix products, arithmetic and copies ran while one was open for 3% of the time, Pallas kernels for 0%

commit v1 on v0

v1 whole, which is shorter than its diff:
```python
import jax
import jax.numpy as jnp
from jax import lax
from jax.experimental import pallas as pl
from jax.experimental.pallas import tpu as pltpu
from jax.sharding import PartitionSpec as P

LO = 256
BF = jnp.bfloat16
F32 = jnp.float32


def split(idx):
    return idx & (LO - 1), idx >> 8


def onehot(lo, width):
    rows = lax.broadcasted_iota(jnp.int32, (LO, width), 0)
    return jnp.where(rows == lo, 1.0, 0.0).astype(BF)


def nn(a, b):
    return jnp.dot(a, b, preferred_element_type=F32)


def nt(a, b):
    return lax.dot_general(a, b, (((1,), (1,)), ((), ())), preferred_element_type=F32)


def tn(a, b):
    return lax.dot_general(a, b, (((0,), (0,)), ((), ())), preferred_element_type=F32)


def pick(res, hi, blocks, feats, base=0):
    acc = jnp.zeros((feats, res.shape[1]), F32)
    for j in range(blocks):
        acc = jnp.where(hi == base + j, res[j * feats:(j + 1) * feats], acc)
    return acc


def params():
    return pltpu.CompilerParams(vmem_limit_bytes=56 * 1024 * 1024)


def full(shape):
    return pl.BlockSpec(shape, lambda i: (0,) * len(shape))


def send_kernel(edges, w_down, send_idx, peers):
    n_edges, width = edges.shape
    feats = w_down.shape[1]
    eb = 512
    nd = n_edges // eb
    per = 4
    ng = peers // per
    slot = send_idx.shape[1] // peers
    blocks = n_edges // LO

    def body(e_ref, w_ref, i_ref, out_ref, table):
        i = pl.program_id(0)

        @pl.when(i < nd)
        def _():
            d = nn(e_ref[...], w_ref[...]).astype(BF).T
            for k in range(eb // LO):
                table[i * (eb // LO) + k] = d[:, k * LO:(k + 1) * LO]

        @pl.when(i >= nd)
        def _():
            tab = table[...].reshape(blocks * feats, LO)
            for a in range(per):
                lo, hi = split(i_ref[:, a * slot:(a + 1) * slot])
                res = nn(tab, onehot(lo, slot))
                out_ref[a] = pick(res, hi, blocks, feats).astype(BF)

    return pl.pallas_call(
        body,
        out_shape=jax.ShapeDtypeStruct((peers, feats, slot), BF),
        grid=(nd + ng,),
        in_specs=[
            pl.BlockSpec((eb, width), lambda i: (jnp.minimum(i, nd - 1), 0)),
            full(w_down.shape),
            pl.BlockSpec((1, per * slot), lambda i: (0, jnp.maximum(i - nd, 0))),
        ],
        out_specs=pl.BlockSpec((per, feats, slot), lambda i: (jnp.maximum(i - nd, 0), 0, 0)),
        scratch_shapes=[pltpu.VMEM((blocks, feats, LO), BF)],
        compiler_params=params(),
        name="send",
    )(edges, w_down, send_idx)


def forward_kernel(recv, src, dst, basis, w_basis_t, n_edges):
    peers, feats, _ = recv.shape
    trips = src.shape[1]
    nb = basis.shape[0]
    tc = 1024
    steps = trips // tc
    eblocks = n_edges // LO

    def body(r_ref, s_ref, d_ref, b_ref, w_ref, src_out, agg_out, acc, pm, oh):
        i = pl.program_id(0)

        @pl.when(i == 0)
        def _():
            acc[...] = jnp.zeros_like(acc)

        tab = r_ref[...].reshape(peers * feats, LO)
        for a in range(tc // LO):
            cols = slice(a * LO, (a + 1) * LO)
            lo, hi = split(s_ref[:, cols])
            source = pick(nn(tab, onehot(lo, LO)), hi, peers, feats)
            src_out[:, cols] = source.astype(BF)
            product = source * nn(w_ref[...], b_ref[:, cols])
            lo, hi = split(d_ref[:, cols])
            for j in range(eblocks):
                pm[j * feats:(j + 1) * feats, cols] = jnp.where(hi == j, product, 0.0).astype(BF)
            oh[:, cols] = onehot(lo, LO)
        acc[...] += nt(pm[...], oh[...])

        @pl.when(i == steps - 1)
        def _():
            for j in range(eblocks):
                agg_out[:, j * LO:(j + 1) * LO] = acc[j * feats:(j + 1) * feats].astype(BF)

    return pl.pallas_call(
        body,
        out_shape=(
            jax.ShapeDtypeStruct((feats, trips), BF),
            jax.ShapeDtypeStruct((feats, n_edges), BF),
        ),
        grid=(steps,),
        in_specs=[
            full(recv.shape),
            pl.BlockSpec((1, tc), lambda i: (0, i)),
            pl.BlockSpec((1, tc), lambda i: (0, i)),
            pl.BlockSpec((nb, tc), lambda i: (0, i)),
            full(w_basis_t.shape),
        ],
        out_specs=(pl.BlockSpec((feats, tc), lambda i: (0, i)), full((feats, n_edges))),
        scratch_shapes=[
            pltpu.VMEM((eblocks * feats, LO), F32),
            pltpu.VMEM((eblocks * feats, tc), BF),
            pltpu.VMEM((LO, tc), BF),
        ],
        compiler_params=params(),
        name="forward",
    )(recv, src, dst, basis, w_basis_t)


def dense_kernel(agg_t, w_up, cot):
    feats, n_edges = agg_t.shape
    width = w_up.shape[1]
    eb = 256
    steps = n_edges // eb

    def body(a_ref, w_ref, c_ref, up_out, g_out):
        i = pl.program_id(0)
        agg = a_ref[...]
        pre = tn(agg, w_ref[...])
        sig = 1.0 / (1.0 + jnp.exp(-pre))
        g_pre = (c_ref[...].astype(F32) * sig * (1.0 + pre * (1.0 - sig))).astype(BF)

        @pl.when(i == 0)
        def _():
            up_out[...] = jnp.zeros_like(up_out)

        up_out[...] += nn(agg, g_pre)
        g_out[...] = nt(w_ref[...], g_pre).astype(BF)

    return pl.pallas_call(
        body,
        out_shape=(
            jax.ShapeDtypeStruct((feats, width), F32),
            jax.ShapeDtypeStruct((feats, n_edges), BF),
        ),
        grid=(steps,),
        in_specs=[
            pl.BlockSpec((feats, eb), lambda i: (0, i)),
            full(w_up.shape),
            pl.BlockSpec((eb, width), lambda i: (i, 0)),
        ],
        out_specs=(full((feats, width)), pl.BlockSpec((feats, eb), lambda i: (0, i))),
        compiler_params=params(),
        name="dense",
    )(agg_t, w_up, cot)


def backward_kernel(g_agg_t, src_t, src, dst, basis, w_basis_t, peers):
    feats, n_edges = g_agg_t.shape
    trips = src.shape[1]
    nb = basis.shape[0]
    tc = 1024
    steps = trips // tc
    eblocks = n_edges // LO

    def body(g_ref, st_ref, s_ref, d_ref, b_ref, w_ref, out_ref, bt_out, table, acc, pm, oh):
        i = pl.program_id(0)

        @pl.when(i == 0)
        def _():
            acc[...] = jnp.zeros_like(acc)
            bt_out[...] = jnp.zeros_like(bt_out)
            for j in range(eblocks):
                table[j * feats:(j + 1) * feats] = g_ref[:, j * LO:(j + 1) * LO]

        for a in range(tc // LO):
            cols = slice(a * LO, (a + 1) * LO)
            lo, hi = split(d_ref[:, cols])
            g_trip = pick(nn(table[...], onehot(lo, LO)), hi, eblocks, feats)
            g_source = g_trip * nn(w_ref[...], b_ref[:, cols])
            g_basis = g_trip * st_ref[:, cols].astype(F32)
            top = g_basis.astype(BF)
            low = (g_basis - top.astype(F32)).astype(BF)
            bt_out[...] += nt(b_ref[:, cols], top) + nt(b_ref[:, cols], low)
            lo, hi = split(s_ref[:, cols])
            for j in range(peers):
                pm[j * feats:(j + 1) * feats, cols] = jnp.where(hi == j, g_source, 0.0).astype(BF)
            oh[:, cols] = onehot(lo, LO)
        acc[...] += nt(pm[...], oh[...])

        @pl.when(i == steps - 1)
        def _():
            out_ref[...] = acc[...].astype(BF).reshape(out_ref.shape)

    return pl.pallas_call(
        body,
        out_shape=(
            jax.ShapeDtypeStruct((peers, feats, LO), BF),
            jax.ShapeDtypeStruct((nb, feats), F32),
        ),
        grid=(steps,),
        in_specs=[
            full(g_agg_t.shape),
            pl.BlockSpec((feats, tc), lambda i: (0, i)),
            pl.BlockSpec((1, tc), lambda i: (0, i)),
            pl.BlockSpec((1, tc), lambda i: (0, i)),
            pl.BlockSpec((nb, tc), lambda i: (0, i)),
            full(w_basis_t.shape),
        ],
        out_specs=(full((peers, feats, LO)), full((nb, feats))),
        scratch_shapes=[
            pltpu.VMEM((eblocks * feats, LO), BF),
            pltpu.VMEM((peers * feats, LO), F32),
            pltpu.VMEM((peers * feats, tc), BF),
            pltpu.VMEM((LO, tc), BF),
        ],
        compiler_params=params(),
        name="backward",
    )(g_agg_t, src_t, src, dst, basis, w_basis_t)


def return_kernel(ret, send_idx, edges):
    peers, feats, slot = ret.shape
    n_edges, width = edges.shape
    per = 8
    steps = peers // per
    eblocks = n_edges // LO
    eb = 512
    esteps = n_edges // eb

    def body(r_ref, i_ref, e_ref, down_out, grad_out, acc, pm, oh, gacc):
        i = pl.program_id(0)

        @pl.when(i == 0)
        def _():
            acc[...] = jnp.zeros_like(acc)
            gacc[...] = jnp.zeros_like(gacc)

        @pl.when(i < steps)
        def _():
            for a in range(per):
                cols = slice(a * slot, (a + 1) * slot)
                lo, hi = split(i_ref[:, cols])
                rows = r_ref[a].astype(F32)
                for j in range(eblocks):
                    pm[j * feats:(j + 1) * feats, cols] = jnp.where(hi == j, rows, 0.0).astype(BF)
                oh[:, cols] = onehot(lo, slot)
            acc[...] += nt(pm[...], oh[...])

        @pl.when(i == steps - 1)
        def _():
            for j in range(eblocks):
                down_out[:, j * LO:(j + 1) * LO] = acc[j * feats:(j + 1) * feats].astype(BF)

        @pl.when(i >= steps)
        def _():
            k = i - steps
            gacc[...] += nn(down_out[:, pl.ds(pl.multiple_of(k * eb, eb), eb)], e_ref[...])

        @pl.when(i == steps + esteps - 1)
        def _():
            grad_out[...] = gacc[...].T.astype(BF)

    return pl.pallas_call(
        body,
        out_shape=(
            jax.ShapeDtypeStruct((feats, n_edges), BF),
            jax.ShapeDtypeStruct((width, feats), BF),
        ),
        grid=(steps + esteps,),
        in_specs=[
            pl.BlockSpec((per, feats, slot), lambda i: (jnp.minimum(i, steps - 1), 0, 0)),
            pl.BlockSpec((1, per * slot), lambda i: (0, jnp.minimum(i, steps - 1))),
            pl.BlockSpec((eb, width), lambda i: (jnp.maximum(i - steps, 0), 0)),
        ],
        out_specs=(full((feats, n_edges)), full((width, feats))),
        scratch_shapes=[
            pltpu.VMEM((eblocks * feats, LO), F32),
            pltpu.VMEM((eblocks * feats, per * slot), BF),
            pltpu.VMEM((LO, per * slot), BF),
            pltpu.VMEM((feats, width), F32),
        ],
        compiler_params=params(),
        name="returned",
    )(ret, send_idx, edges)


def edges_kernel(g_down_t, w_down_t):
    feats, n_edges = g_down_t.shape
    width = w_down_t.shape[1]
    eb = 512

    def body(g_ref, w_ref, out_ref):
        out_ref[...] = tn(g_ref[...], w_ref[...]).astype(BF)

    return pl.pallas_call(
        body,
        out_shape=jax.ShapeDtypeStruct((n_edges, width), BF),
        grid=(n_edges // eb,),
        in_specs=[pl.BlockSpec((feats, eb), lambda i: (0, i)), full(w_down_t.shape)],
        out_specs=pl.BlockSpec((eb, width), lambda i: (i, 0)),
        compiler_params=params(),
        name="grad_edges",
    )(g_down_t, w_down_t)


def exchange(x, axes):
    return lax.all_to_all(x, axes, split_axis=0, concat_axis=0, tiled=True)


def reduce_all(x, n):
    rows, feats = x.shape
    mine = exchange(x, ("dp", "graph")).reshape(n, rows // n, feats).astype(F32).sum(axis=0)
    spread = jnp.broadcast_to(mine.astype(BF)[None], (n,) + mine.shape).reshape(rows, feats)
    return exchange(spread, ("dp", "graph"))


def make_shards(n_dp, n_graph):
    n = n_dp * n_graph

    def shards(edges, send_rows, trip_src, trip_dst, basis_values, cotangent, w_down, w_up, w_basis):
        edge_rows = edges[0]
        basis = basis_values[0]
        n_edges, width = edge_rows.shape
        feats = w_down.shape[1]
        nb = basis.shape[0]
        w_basis_t = w_basis.T
        sent = send_kernel(edge_rows, w_down, send_rows, n_graph)
        received = exchange(sent, "graph")
        src_t, agg_t = forward_kernel(received, trip_src, trip_dst, basis, w_basis_t, n_edges)
        up_term, g_agg_t = dense_kernel(agg_t, w_up, cotangent[0])
        g_received, basis_term = backward_kernel(
            g_agg_t, src_t, trip_src, trip_dst, basis, w_basis_t, n_graph
        )
        returned = exchange(g_received, "graph")
        pad = -nb % n
        small = jnp.concatenate(
            [up_term.reshape(width, feats), basis_term, jnp.zeros((pad, feats), F32)]
        ).astype(BF)
        reduced = reduce_all(small, n).astype(F32)
        g_down_t, down_term = return_kernel(returned, send_rows, edge_rows)
        grad_down = reduce_all(down_term, n).astype(F32)
        grad_edges = edges_kernel(g_down_t, w_down.T)
        grad_up = reduced[:width].reshape(feats, width)
        grad_basis = reduced[width:width + nb]
        return grad_edges[None], grad_down, grad_up, grad_basis

    return shards


def solution(mesh):
    shape = dict(mesh.shape)
    in_specs = (
        P("dp", "graph", None),
        P("dp", "graph"),
        P("dp", "graph"),
        P("dp", "graph"),
        P("dp", None, "graph"),
        P("dp", "graph", None),
        P(),
        P(),
        P(),
    )
    out_specs = (P("dp", "graph", None), P(), P(), P())
    return jax.shard_map(
        make_shards(shape["dp"], shape["graph"]),
        mesh=mesh,
        in_specs=in_specs,
        out_specs=out_specs,
        check_vma=False,
    )
```

time: 686 us -> 309 us (0.45)
  other arithmetic: 151 us -> 1.42 us
  waiting for transfers between devices: 300 us -> 151 us
  Pallas kernels: 0 us -> 101 us
  local copies, waits for them, and re-layouts: 87.8 us -> 7.71 us
  blocking collectives: 79.8 us -> 0 us
  matrix products: 32.5 us -> 0 us
  starting transfers between devices: 19.2 us -> 46.7 us
  between operations: 14.3 us -> 0.79 us
    psum x1 -> x0, waiting for transfers between devices: 165 us -> none  [shards(): lax.psum((down_term, up_term, basis_term), ('dp', 'graph'))]
    scatter-add x3 -> x0, other arithmetic: 146 us -> none  [the longest x1 51.4 us: shards(): jax.ops.segment_sum(g_source, source_index, num_segments=asked_rows)]
    pallas_call x0 -> x6, Pallas kernels: none -> 101 us  [the longest x1 33.6 us: backward_kernel(): pl.pallas_call(body, out_shape=(jax.ShapeDtypeStruct((peers, feats, LO),...]
    gather x3 -> x0, local copies, waits for them, and re-layouts: 81.3 us -> none  [the longest x1 29.4 us: shards(): source_rows = jnp.take(received, source_index, axis=0).astype(jnp.float32)]
    psum x1 -> x0, blocking collectives: 79.8 us -> none  [shards(): lax.psum((down_term, up_term, basis_term), ('dp', 'graph'))]
    dot_general x8 -> x0, matrix products: 32.5 us -> none  [the longest x1 7.05 us: shards(): jnp.dot(basis_block.astype(jnp.float32), g_basis_emb, precision=lax.Preci...]
    all_to_all x2 -> x6, starting transfers between devices: 19.2 us -> 46.7 us  [exchange(): return lax.all_to_all(x, axes, split_axis=0, concat_axis=0, tiled=True)]
    all_to_all x2 -> x6, waiting for transfers between devices: 135 us -> 151 us  [exchange(): return lax.all_to_all(x, axes, split_axis=0, concat_axis=0, tiled=True)]
  transfers between devices with their start and end apart: 3 -> 6, of which waited for: 3 -> 6; matrix products, arithmetic and copies ran while one was open for 3% -> 2% of each run, Pallas kernels for 0% -> 5%
where the time goes in v1:
time: 309 us; the launch traced here: 308 us
  waiting for transfers between devices  151 us (49%)
  Pallas kernels  101 us (33%)
  starting transfers between devices  46.7 us (15%)
  local copies, waits for them, and re-layouts  7.71 us (2%)
    all_to_all x6, waiting for transfers between devices, exchange(): return lax.all_to_all(x, axes, split_axis=0, concat_axis=0, tiled=True)  151 us
    all_to_all x6, starting transfers between devices, exchange(): return lax.all_to_all(x, axes, split_axis=0, concat_axis=0, tiled=True)  46.7 us
    pallas_call x1, Pallas kernels, backward_kernel(): pl.pallas_call(body, out_shape=(jax.ShapeDtypeStruct((peers, feats, LO),...  33.6 us
    pallas_call x1, Pallas kernels, forward_kernel(): pl.pallas_call(body, out_shape=(jax.ShapeDtypeStruct((feats, trips), BF),...  29.7 us
    pallas_call x1, Pallas kernels, return_kernel(): pl.pallas_call(body, out_shape=(jax.ShapeDtypeStruct((feats, n_edges), BF...  11.1 us
    pallas_call x1, Pallas kernels, send_kernel(): pl.pallas_call(body, out_shape=jax.ShapeDtypeStruct((peers, feats, slot),...  10.9 us
    pallas_call x1, Pallas kernels, dense_kernel(): pl.pallas_call(body, out_shape=(jax.ShapeDtypeStruct((feats, width), F32)...  10.6 us
  transfers between devices with their start and end apart: 6, of which 6 were waited for; matrix products, arithmetic and copies ran while one was open for 2% of the time, Pallas kernels for 5%

profile of v1, /device:TPU:1, one launch (start us, length us, event | category | flops | bytes accessed | tf_op | source)
XLA Modules:
  0.0 308.3 jit_solution(3981521361679086890)
XLA Ops:
  0.6 10.9 %send.1 = bf16[32,128,256]{2,1,0:T(8,128)(2,1)} custom-call(bf16[2048,1024]{1,0:T(8,128)(2,1)} %bitcast.9, bf16[1024,128]{1,0:T(8,128)(2,1)} %w_ref.2, s32[1,8192]{1,0:T(1,128)} %i_ref.3), custom_call_target="tpu_custom_call" | custom-call | tf_op jit(solution)/shard_map/send/pallas_call | solution.py:76
  11.6 12.2 %all-to-all-start = ((bf16[32,128,256]{2,1,0:T(8,128)(2,1)}), bf16[32,128,256]{2,1,0:T(8,128)(2,1)S(1)}, u32[]{:S(2)}, u32[]{:S(2)}) async-start(bf16[32,128,256]{2,1,0:T(8,128)(2,1)} %send.1), calls=%async_computation | async-start | bytes 4194304 | tf_op jit(solution)/shard_map/all_to_all | solution.py:338
  24.5 48.1 %all-to-all-done.r_ref = bf16[32,128,256]{2,1,0:T(8,128)(2,1)S(1)} async-done(((bf16[32,128,256]{2,1,0:T(8,128)(2,1)}), bf16[32,128,256]{2,1,0:T(8,128)(2,1)S(1)}, u32[]{:S(2)}, u32[]{:S(2)}) %all-to-all-start) | async-done | bytes 2097184 | tf_op jit(solution)/shard_map/all_to_all | solution.py:338
  72.6 1.3 copy-done.1
  73.9 29.7 %forward.1 = (bf16[128,8192]{1,0:T(8,128)(2,1)}, bf16[128,2048]{1,0:T(8,128)(2,1)}) custom-call(bf16[32,128,256]{2,1,0:T(8,128)(2,1)} %copy-done.1, s32[1,8192]{1,0:T(1,128)} %s_ref.3, s32[1,8192]{1,0:T(1,128)} %d_ref.3, bf16[42,8192]{1,0:T(8,128)(2,1)} %bitcast.13, bf16[128,42]{1,0:T(8,128)(2,1)} %bitcast.17), custom_call_target="tpu_custom_call" | custom-call | tf_op jit(solution)/shard_map/forward/pallas_call | solution.py:125
  103.7 10.6 %dense.1 = (f32[128,1024]{1,0:T(8,128)}, bf16[128,2048]{1,0:T(8,128)(2,1)}) custom-call(bf16[128,2048]{1,0:T(8,128)(2,1)} %get-tuple-element.12.a_ref, bf16[128,1024]{1,0:T(8,128)(2,1)} %w_ref.3, bf16[2048,1024]{1,0:T(8,128)(2,1)} %bitcast.11), custom_call_target="tpu_custom_call" | custom-call | tf_op jit(solution)/shard_map/dense/pallas_call | solution.py:170
  114.3 33.6 %backward.1 = (bf16[32,128,256]{2,1,0:T(8,128)(2,1)}, f32[42,128]{1,0:T(8,128)}) custom-call(bf16[128,2048]{1,0:T(8,128)(2,1)} %get-tuple-element.13.g_ref, bf16[128,8192]{1,0:T(8,128)(2,1)} %get-tuple-element.14.st_ref, s32[1,8192]{1,0:T(1,128)} %s_ref.3, s32[1,8192]{1,0:T(1,128)} %d_ref.3, bf16[42,8192]{1,0:T(8,128)(2,1)} %bitcast.14, bf16[128,42]{1,0:T(8,128)(2,1)} %bitcast.18), custom_call_target="tpu_custom_call" | custom-call | tf_op jit(solution)/shard_map/backward/pallas_call | solution.py:225
  147.9 7.2 %all-to-all-start.1 = ((bf16[32,128,256]{2,1,0:T(8,128)(2,1)}), bf16[32,128,256]{2,1,0:T(8,128)(2,1)S(1)}, u32[]{:S(2)}, u32[]{:S(2)}) async-start(bf16[32,128,256]{2,1,0:T(8,128)(2,1)} %get-tuple-element.15), calls=%async_computation.1 | async-start | bytes 4194304 | tf_op jit(solution)/shard_map/all_to_all | solution.py:338
  155.8 0.9 convert_element_type.23
  156.7 47.0 %all-to-all-done.1.r_ref = bf16[32,128,256]{2,1,0:T(8,128)(2,1)S(1)} async-done(((bf16[32,128,256]{2,1,0:T(8,128)(2,1)}), bf16[32,128,256]{2,1,0:T(8,128)(2,1)S(1)}, u32[]{:S(2)}, u32[]{:S(2)}) %all-to-all-start.1) | async-done | bytes 2097184 | tf_op jit(solution)/shard_map/all_to_all | solution.py:338
  203.8 11.1 %all-to-all-start.4 = ((bf16[256,5,128]{2,1,0:T(8,128)(2,1)}), bf16[256,5,128]{2,1,0:T(8,128)(2,1)S(1)}, u32[]{:S(2)}, u32[]{:S(2)}) async-start(bf16[256,5,128]{2,1,0:T(8,128)(2,1)} %convert_element_type.23), calls=%async_computation.4 | async-start | bytes 1048576 | tf_op jit(solution)/shard_map/all_to_all | solution.py:338
  214.9 11.1 %returned.1 = (bf16[128,2048]{1,0:T(8,128)(2,1)}, bf16[1024,128]{1,0:T(8,128)(2,1)}) custom-call(bf16[32,128,256]{2,1,0:T(8,128)(2,1)} %copy-done, s32[1,8192]{1,0:T(1,128)} %i_ref.3, bf16[2048,1024]{1,0:T(8,128)(2,1)} %bitcast.10), custom_call_target="tpu_custom_call" | custom-call | tf_op jit(solution)/shard_map/returned/pallas_call | solution.py:294
  226.0 10.3 %all-to-all-done.4 = bf16[256,5,128]{2,1,0:T(8,128)(2,1)S(1)} async-done(((bf16[256,5,128]{2,1,0:T(8,128)(2,1)}), bf16[256,5,128]{2,1,0:T(8,128)(2,1)S(1)}, u32[]{:S(2)}, u32[]{:S(2)}) %all-to-all-start.4) | async-done | bytes 327712 | tf_op jit(solution)/shard_map/all_to_all | solution.py:338
  236.3 5.4 %all-to-all-start.2 = ((bf16[256,4,128]{2,1,0:T(4,128)(2,1)}), bf16[256,4,128]{2,1,0:T(4,128)(2,1)S(1)}, u32[]{:S(2)}, u32[]{:S(2)}) async-start(bf16[256,4,128]{2,1,0:T(4,128)(2,1)} %bitcast.19), calls=%async_computation.2 | async-start | bytes 524288 | tf_op jit(solution)/shard_map/all_to_all | solution.py:338
  242.0 15.6 %all-to-all-done.2 = bf16[256,4,128]{2,1,0:T(4,128)(2,1)S(1)} async-done(((bf16[256,4,128]{2,1,0:T(4,128)(2,1)}), bf16[256,4,128]{2,1,0:T(4,128)(2,1)S(1)}, u32[]{:S(2)}, u32[]{:S(2)}) %all-to-all-start.2) | async-done | bytes 262176 | tf_op jit(solution)/shard_map/all_to_all | solution.py:338
  257.6 0.9 broadcast_in_dim.21
  258.4 5.4 %all-to-all-start.5 = ((bf16[256,5,128]{2,1,0:T(8,128)(2,1)}), bf16[256,5,128]{2,1,0:T(8,128)(2,1)S(1)}, u32[]{:S(2)}, u32[]{:S(2)}) async-start(bf16[256,5,128]{2,1,0:T(8,128)(2,1)} %broadcast_in_dim.21), calls=%async_computation.5 | async-start | bytes 1048576 | tf_op jit(solution)/shard_map/all_to_all | solution.py:338
  264.2 21.2 %all-to-all-done.5 = bf16[256,5,128]{2,1,0:T(8,128)(2,1)S(1)} async-done(((bf16[256,5,128]{2,1,0:T(8,128)(2,1)}), bf16[256,5,128]{2,1,0:T(8,128)(2,1)S(1)}, u32[]{:S(2)}, u32[]{:S(2)}) %all-to-all-start.5) | async-done | bytes 327712 | tf_op jit(solution)/shard_map/all_to_all | solution.py:338
  286.2 5.4 %all-to-all-start.3 = ((bf16[256,4,128]{2,1,0:T(4,128)(2,1)}), bf16[256,4,128]{2,1,0:T(4,128)(2,1)S(1)}, u32[]{:S(2)}, u32[]{:S(2)}) async-start(bf16[256,4,128]{2,1,0:T(4,128)(2,1)} %broadcast_in_dim.9), calls=%async_computation.3 | async-start | bytes 524288 | tf_op jit(solution)/shard_map/all_to_all | solution.py:338
  291.6 0.8 copy.16
  293.2 0.9 reshape.40
  294.1 4.8 %grad_edges.1 = bf16[2048,1024]{1,0:T(8,128)(2,1)} custom-call(bf16[128,2048]{1,0:T(8,128)(2,1)} %get-tuple-element.16.g_ref, bf16[128,1024]{1,0:T(8,128)(2,1)} %bitcast.16), custom_call_target="tpu_custom_call" | custom-call | tf_op jit(solution)/shard_map/grad_edges/pallas_call | solution.py:326
  298.9 8.6 %all-to-all-done.3 = bf16[256,4,128]{2,1,0:T(4,128)(2,1)S(1)} async-done(((bf16[256,4,128]{2,1,0:T(4,128)(2,1)}), bf16[256,4,128]{2,1,0:T(4,128)(2,1)S(1)}, u32[]{:S(2)}, u32[]{:S(2)}) %all-to-all-start.3) | async-done | bytes 262176 | tf_op jit(solution)/shard_map/all_to_all | solution.py:338
  307.5 0.8 convert.15
  (23 shorter events, 3.5 us)
Async XLA Ops:
  11.6 12.2 %copy-start.5 = (bf16[42,128]{1,0:T(8,128)(2,1)S(1)}, bf16[42,128]{1,0:T(8,128)(2,1)}, u32[]{:S(2)}) copy-start(bf16[42,128]{1,0:T(8,128)(2,1)} %param.17) | copy-start | bytes 32260
  11.6 61.0 %all-to-all-start = ((bf16[32,128,256]{2,1,0:T(8,128)(2,1)}), bf16[32,128,256]{2,1,0:T(8,128)(2,1)S(1)}, u32[]{:S(2)}, u32[]{:S(2)}) async-start(bf16[32,128,256]{2,1,0:T(8,128)(2,1)} %send.1), calls=%async_computation | async-start | bytes 4194304 | tf_op jit(solution)/shard_map/all_to_all | solution.py:338
  72.6 1.3 copy-start.1
  147.9 7.2 %copy-start.4 = (f32[42,128]{1,0:T(8,128)S(1)}, f32[42,128]{1,0:T(8,128)}, u32[]{:S(2)}) copy-start(f32[42,128]{1,0:T(8,128)} %get-tuple-element.19) | copy-start | bytes 64516
  147.9 7.2 %copy-start.3 = (f32[128,1024]{1,0:T(8,128)S(1)}, f32[128,1024]{1,0:T(8,128)}, u32[]{:S(2)}) copy-start(f32[128,1024]{1,0:T(8,128)} %get-tuple-element.18) | copy-start | bytes 1572868
  147.9 55.8 %all-to-all-start.1 = ((bf16[32,128,256]{2,1,0:T(8,128)(2,1)}), bf16[32,128,256]{2,1,0:T(8,128)(2,1)S(1)}, u32[]{:S(2)}, u32[]{:S(2)}) async-start(bf16[32,128,256]{2,1,0:T(8,128)(2,1)} %get-tuple-element.15), calls=%async_computation.1 | async-start | bytes 4194304 | tf_op jit(solution)/shard_map/all_to_all | solution.py:338
  203.8 11.2 %copy-start = (bf16[32,128,256]{2,1,0:T(8,128)(2,1)}, bf16[32,128,256]{2,1,0:T(8,128)(2,1)S(1)}, u32[]{:S(2)}) copy-start(bf16[32,128,256]{2,1,0:T(8,128)(2,1)S(1)} %all-to-all-done.1.r_ref) | copy-start | bytes 6291460
  203.8 32.5 %all-to-all-start.4 = ((bf16[256,5,128]{2,1,0:T(8,128)(2,1)}), bf16[256,5,128]{2,1,0:T(8,128)(2,1)S(1)}, u32[]{:S(2)}, u32[]{:S(2)}) async-start(bf16[256,5,128]{2,1,0:T(8,128)(2,1)} %convert_element_type.23), calls=%async_computation.4 | async-start | bytes 1048576 | tf_op jit(solution)/shard_map/all_to_all | solution.py:338
  226.0 65.6 %copy-start.2 = (bf16[1024,128]{1,0:T(8,128)(2,1)S(1)}, bf16[1024,128]{1,0:T(8,128)(2,1)}, u32[]{:S(2)}) copy-start(bf16[1024,128]{1,0:T(8,128)(2,1)} %w_ref.2) | copy-start | bytes 786436
  236.3 21.3 %all-to-all-start.2 = ((bf16[256,4,128]{2,1,0:T(4,128)(2,1)}), bf16[256,4,128]{2,1,0:T(4,128)(2,1)S(1)}, u32[]{:S(2)}, u32[]{:S(2)}) async-start(bf16[256,4,128]{2,1,0:T(4,128)(2,1)} %bitcast.19), calls=%async_computation.2 | async-start | bytes 524288 | tf_op jit(solution)/shard_map/all_to_all | solution.py:338
  258.4 26.9 %all-to-all-start.5 = ((bf16[256,5,128]{2,1,0:T(8,128)(2,1)}), bf16[256,5,128]{2,1,0:T(8,128)(2,1)S(1)}, u32[]{:S(2)}, u32[]{:S(2)}) async-start(bf16[256,5,128]{2,1,0:T(8,128)(2,1)} %broadcast_in_dim.21), calls=%async_computation.5 | async-start | bytes 1048576 | tf_op jit(solution)/shard_map/all_to_all | solution.py:338
  286.2 21.3 %all-to-all-start.3 = ((bf16[256,4,128]{2,1,0:T(4,128)(2,1)}), bf16[256,4,128]{2,1,0:T(4,128)(2,1)S(1)}, u32[]{:S(2)}, u32[]{:S(2)}) async-start(bf16[256,4,128]{2,1,0:T(4,128)(2,1)} %broadcast_in_dim.9), calls=%async_computation.3 | async-start | bytes 524288 | tf_op jit(solution)/shard_map/all_to_all | solution.py:338

commit v2 on v1

v2 whole, which is shorter than its diff:
```python
import jax
import jax.numpy as jnp
from jax import lax
from jax.experimental import pallas as pl
from jax.experimental.pallas import tpu as pltpu
from jax.sharding import PartitionSpec as P

LO = 256
BF = jnp.bfloat16
F32 = jnp.float32


def split(idx):
    return idx & (LO - 1), idx >> 8


def onehot(lo, width):
    rows = lax.broadcasted_iota(jnp.int32, (LO, width), 0)
    return jnp.where(rows == lo, 1.0, 0.0).astype(BF)


def nn(a, b):
    return jnp.dot(a, b, preferred_element_type=F32)


def nt(a, b):
    return lax.dot_general(a, b, (((1,), (1,)), ((), ())), preferred_element_type=F32)


def tn(a, b):
    return lax.dot_general(a, b, (((0,), (0,)), ((), ())), preferred_element_type=F32)


def pick(res, hi, blocks, feats, base=0):
    acc = jnp.zeros((feats, res.shape[1]), F32)
    for j in range(blocks):
        acc = jnp.where(hi == base + j, res[j * feats:(j + 1) * feats], acc)
    return acc


def params():
    return pltpu.CompilerParams(vmem_limit_bytes=56 * 1024 * 1024)


def full(shape):
    return pl.BlockSpec(shape, lambda i: (0,) * len(shape))


def send_kernel(edges, w_down, send_idx, peers):
    n_edges, width = edges.shape
    feats = w_down.shape[1]
    eb = 512
    nd = n_edges // eb
    per = 4
    ng = peers // per
    slot = send_idx.shape[1] // peers
    blocks = n_edges // LO

    def body(e_ref, w_ref, i_ref, out_ref, table):
        i = pl.program_id(0)

        @pl.when(i < nd)
        def _():
            d = nn(e_ref[...], w_ref[...]).astype(BF).T
            for k in range(eb // LO):
                table[i * (eb // LO) + k] = d[:, k * LO:(k + 1) * LO]

        @pl.when(i >= nd)
        def _():
            tab = table[...].reshape(blocks * feats, LO)
            for a in range(per):
                lo, hi = split(i_ref[:, a * slot:(a + 1) * slot])
                res = nn(tab, onehot(lo, slot))
                out_ref[a] = pick(res, hi, blocks, feats).astype(BF)

    return pl.pallas_call(
        body,
        out_shape=jax.ShapeDtypeStruct((peers, feats, slot), BF),
        grid=(nd + ng,),
        in_specs=[
            pl.BlockSpec((eb, width), lambda i: (jnp.minimum(i, nd - 1), 0)),
            full(w_down.shape),
            pl.BlockSpec((1, per * slot), lambda i: (0, jnp.maximum(i - nd, 0))),
        ],
        out_specs=pl.BlockSpec((per, feats, slot), lambda i: (jnp.maximum(i - nd, 0), 0, 0)),
        scratch_shapes=[pltpu.VMEM((blocks, feats, LO), BF)],
        compiler_params=params(),
        name="send",
    )(edges, w_down, send_idx)


def sort_kernel(src, dst, basis, peers):
    trips = src.shape[1]
    nb = basis.shape[0]
    rows = -(-(nb + 4) // 16) * 16
    chunks = trips // LO
    tc = 1024
    steps = trips // tc

    def body(s_ref, d_ref, b_ref, x_out, range_out, oh_hi, first, pm, oh, acc):
        i = pl.program_id(0)

        @pl.when(i == 0)
        def _():
            acc[...] = jnp.zeros_like(acc)
            bucket = lax.broadcasted_iota(jnp.int32, (peers, trips), 0)
            hot = jnp.where(bucket == (s_ref[...] >> 8), 1.0, 0.0)
            oh_hi[...] = hot.astype(BF)
            total = jnp.broadcast_to(jnp.sum(hot, axis=1, keepdims=True), (peers, 128))
            high = jnp.floor(total * (1.0 / 256.0))
            low = total - high * 256.0
            r = lax.broadcasted_iota(jnp.int32, (peers, peers), 0)
            c = lax.broadcasted_iota(jnp.int32, (peers, peers), 1)
            before = jnp.where(c < r, 1.0, 0.0).astype(BF)
            start = 256.0 * nn(before, high.astype(BF)) + nn(before, low.astype(BF))
            first[...] = start
            edge = 256.0 * lax.broadcasted_iota(jnp.int32, (peers, 128), 1).astype(F32)
            b0 = jnp.sum(jnp.where(start + total <= edge, 1.0, 0.0), axis=0, keepdims=True)
            b1 = jnp.sum(jnp.where(start < edge + 256.0, 1.0, 0.0), axis=0, keepdims=True) - 1.0
            range_out[0:1] = jnp.minimum(b0, peers - 1.0).astype(jnp.int32)
            range_out[1:2] = b1.astype(jnp.int32)

        r = lax.broadcasted_iota(jnp.int32, (LO, LO), 0)
        c = lax.broadcasted_iota(jnp.int32, (LO, LO), 1)
        upto = jnp.where(r <= c, 1.0, 0.0).astype(BF)
        for a in range(tc // LO):
            cols = slice(a * LO, (a + 1) * LO)
            at = pl.multiple_of(i * tc + a * LO, LO)
            hot = oh_hi[:, pl.ds(at, LO)]
            count = nn(hot, upto)
            place = first[:, 0:1] + count - 1.0
            hot32 = hot.astype(F32)
            pos = jnp.sum(hot32 * place, axis=0, keepdims=True).astype(jnp.int32)
            first[...] += jnp.broadcast_to(count[:, LO - 1:LO], first.shape)
            s_lo, s_hi = split(s_ref[:, pl.ds(at, LO)])
            d_lo, d_hi = split(d_ref[:, cols])
            row = lax.broadcasted_iota(jnp.int32, (rows - nb, LO), 0)
            extra = jnp.where(row == 0, s_lo, jnp.where(row == 1, s_hi, jnp.where(row == 2, d_lo, jnp.where(row == 3, d_hi, 0))))
            x = jnp.concatenate([b_ref[:, cols].astype(F32), extra.astype(F32)], axis=0)
            lo, hi = split(pos)
            for j in range(chunks):
                pm[j * rows:(j + 1) * rows, cols] = jnp.where(hi == j, x, 0.0).astype(BF)
            oh[:, cols] = onehot(lo, LO)
        acc[...] += nt(pm[...], oh[...])

        @pl.when(i == steps - 1)
        def _():
            x_out[...] = acc[...].reshape(x_out.shape)

    return pl.pallas_call(
        body,
        out_shape=(
            jax.ShapeDtypeStruct((chunks, rows, LO), F32),
            jax.ShapeDtypeStruct((2, 128), jnp.int32),
        ),
        grid=(steps,),
        in_specs=[
            full(src.shape),
            pl.BlockSpec((1, tc), lambda i: (0, i)),
            pl.BlockSpec((nb, tc), lambda i: (0, i)),
        ],
        out_specs=(full((chunks, rows, LO)), full((2, 128))),
        scratch_shapes=[
            pltpu.VMEM((peers, trips), BF),
            pltpu.VMEM((peers, 128), F32),
            pltpu.VMEM((chunks * rows, tc), BF),
            pltpu.VMEM((LO, tc), BF),
            pltpu.VMEM((chunks * rows, LO), F32),
        ],
        compiler_params=params(),
        name="order",
    )(src, dst, basis)


NEAR = 3


def forward_kernel(recv, ranges, trip, w_basis_t, n_edges, nb):
    peers, feats, _ = recv.shape
    chunks, rows, _ = trip.shape
    per = 8
    steps = chunks // per
    eblocks = n_edges // LO

    def body(rg, r_ref, x_ref, w_ref, src_out, agg_out, acc, pm, oh, source):
        i = pl.program_id(0)

        @pl.when(i == 0)
        def _():
            acc[...] = jnp.zeros_like(acc)

        def ids(a, k):
            return x_ref[a, nb + k:nb + k + 1].astype(jnp.int32)

        far = jnp.int32(0)
        for a in range(per):
            b0 = rg[0, i * per + a]
            far = jnp.maximum(far, rg[1, i * per + a] - b0)
            hot = onehot(ids(a, 0), LO)
            hi = ids(a, 1)
            got = jnp.zeros((feats, LO), F32)
            for n in range(NEAR):
                res = nn(r_ref[jnp.minimum(b0 + n, peers - 1)], hot)
                got = jnp.where(hi == b0 + n, res, got)
            source[a] = got

        @pl.when(far >= NEAR)
        def _():
            for a in range(per):
                def more(b, _, a=a):
                    res = nn(r_ref[b], onehot(ids(a, 0), LO))
                    source[a] = jnp.where(ids(a, 1) == b, res, source[a])
                    return 0
                lax.fori_loop(rg[0, i * per + a] + NEAR, rg[1, i * per + a] + 1, more, 0)

        for a in range(per):
            cols = slice(a * LO, (a + 1) * LO)
            src_out[a] = source[a].astype(BF)
            product = source[a] * nn(w_ref[...], x_ref[a].astype(BF))
            hi = ids(a, 3)
            for j in range(eblocks):
                pm[j * feats:(j + 1) * feats, cols] = jnp.where(hi == j, product, 0.0).astype(BF)
            oh[:, cols] = onehot(ids(a, 2), LO)
        acc[...] += nt(pm[...], oh[...])

        @pl.when(i == steps - 1)
        def _():
            for j in range(eblocks):
                agg_out[:, j * LO:(j + 1) * LO] = acc[j * feats:(j + 1) * feats].astype(BF)

    def whole(shape):
        return pl.BlockSpec(shape, lambda i, rg: (0,) * len(shape))

    return pl.pallas_call(
        body,
        out_shape=(
            jax.ShapeDtypeStruct((chunks, feats, LO), BF),
            jax.ShapeDtypeStruct((feats, n_edges), BF),
        ),
        grid_spec=pltpu.PrefetchScalarGridSpec(
            num_scalar_prefetch=1,
            grid=(steps,),
            in_specs=[
                whole(recv.shape),
                pl.BlockSpec((per, rows, LO), lambda i, rg: (i, 0, 0)),
                whole(w_basis_t.shape),
            ],
            out_specs=(
                pl.BlockSpec((per, feats, LO), lambda i, rg: (i, 0, 0)),
                whole((feats, n_edges)),
            ),
            scratch_shapes=[
                pltpu.VMEM((eblocks * feats, LO), F32),
                pltpu.VMEM((eblocks * feats, per * LO), BF),
                pltpu.VMEM((LO, per * LO), BF),
                pltpu.VMEM((per, feats, LO), F32),
            ],
        ),
        compiler_params=params(),
        name="forward",
    )(ranges, recv, trip, w_basis_t)


def dense_kernel(agg_t, w_up, cot):
    feats, n_edges = agg_t.shape
    width = w_up.shape[1]
    eb = 256
    steps = n_edges // eb

    def body(a_ref, w_ref, c_ref, p_out, g_out):
        pre = tn(a_ref[...], w_ref[...])
        t = 0.5 * jnp.tanh(0.5 * pre)
        g_pre = (c_ref[...].astype(F32) * (0.5 + t) * (1.0 + pre * (0.5 - t))).astype(BF)
        p_out[...] = g_pre
        g_out[...] = nt(w_ref[...], g_pre).astype(BF)

    return pl.pallas_call(
        body,
        out_shape=(
            jax.ShapeDtypeStruct((n_edges, width), BF),
            jax.ShapeDtypeStruct((feats, n_edges), BF),
        ),
        grid=(steps,),
        in_specs=[
            pl.BlockSpec((feats, eb), lambda i: (0, i)),
            full(w_up.shape),
            pl.BlockSpec((eb, width), lambda i: (i, 0)),
        ],
        out_specs=(
            pl.BlockSpec((eb, width), lambda i: (i, 0)),
            pl.BlockSpec((feats, eb), lambda i: (0, i)),
        ),
        compiler_params=params(),
        name="dense",
    )(agg_t, w_up, cot)


def backward_kernel(g_agg_t, src_t, ranges, trip, w_basis_t, peers, nb):
    feats, n_edges = g_agg_t.shape
    chunks, rows, _ = trip.shape
    per = 8
    steps = chunks // per
    eblocks = n_edges // LO

    def body(rg, g_ref, st_ref, x_ref, w_ref, out_ref, gb_out, table, acc, source):
        i = pl.program_id(0)

        @pl.when(i == 0)
        def _():
            acc[...] = jnp.zeros_like(acc)
            for j in range(eblocks):
                table[j * feats:(j + 1) * feats] = g_ref[:, j * LO:(j + 1) * LO]

        def ids(a, k):
            return x_ref[a, nb + k:nb + k + 1].astype(jnp.int32)

        far = jnp.int32(0)
        for a in range(per):
            g_trip = pick(nn(table[...], onehot(ids(a, 2), LO)), ids(a, 3), eblocks, feats)
            gb_out[a] = g_trip * st_ref[a].astype(F32)
            source[a] = g_trip * nn(w_ref[...], x_ref[a].astype(BF))
        for a in range(per):
            b0 = rg[0, i * per + a]
            far = jnp.maximum(far, rg[1, i * per + a] - b0)
            hot = onehot(ids(a, 0), LO)
            hi = ids(a, 1)
            for n in range(NEAR):
                res = nt(jnp.where(hi == b0 + n, source[a], 0.0).astype(BF), hot)
                acc[jnp.minimum(b0 + n, peers - 1)] += res

        @pl.when(far >= NEAR)
        def _():
            for a in range(per):
                def more(b, _, a=a):
                    part = jnp.where(ids(a, 1) == b, source[a], 0.0).astype(BF)
                    acc[b] += nt(part, onehot(ids(a, 0), LO))
                    return 0
                lax.fori_loop(rg[0, i * per + a] + NEAR, rg[1, i * per + a] + 1, more, 0)

        @pl.when(i == steps - 1)
        def _():
            out_ref[...] = acc[...].astype(BF)

    def whole(shape):
        return pl.BlockSpec(shape, lambda i, rg: (0,) * len(shape))

    return pl.pallas_call(
        body,
        out_shape=(
            jax.ShapeDtypeStruct((peers, feats, LO), BF),
            jax.ShapeDtypeStruct((chunks, feats, LO), F32),
        ),
        grid_spec=pltpu.PrefetchScalarGridSpec(
            num_scalar_prefetch=1,
            grid=(steps,),
            in_specs=[
                whole(g_agg_t.shape),
                pl.BlockSpec((per, feats, LO), lambda i, rg: (i, 0, 0)),
                pl.BlockSpec((per, rows, LO), lambda i, rg: (i, 0, 0)),
                whole(w_basis_t.shape),
            ],
            out_specs=(
                whole((peers, feats, LO)),
                pl.BlockSpec((per, feats, LO), lambda i, rg: (i, 0, 0)),
            ),
            scratch_shapes=[
                pltpu.VMEM((eblocks * feats, LO), BF),
                pltpu.VMEM((peers, feats, LO), F32),
                pltpu.VMEM((per, feats, LO), F32),
            ],
        ),
        compiler_params=params(),
        name="backward",
    )(ranges, g_agg_t, src_t, trip, w_basis_t)


def weights_kernel(agg_t, g_pre, g_basis, trip, fold):
    feats, n_edges = agg_t.shape
    width = g_pre.shape[1]
    chunks, rows, _ = trip.shape
    steps = 4
    eb = n_edges // steps
    per = chunks // steps
    per_row = width // fold

    def body(a_ref, p_ref, g_ref, x_ref, out_ref, up, bt):
        i = pl.program_id(0)

        @pl.when(i == 0)
        def _():
            up[...] = jnp.zeros_like(up)
            bt[...] = jnp.zeros_like(bt)

        up[...] += nn(a_ref[...], p_ref[...])
        for a in range(per):
            top = g_ref[a].astype(BF)
            low = (g_ref[a] - top.astype(F32)).astype(BF)
            basis = x_ref[a].astype(BF)
            bt[...] += nt(basis, top) + nt(basis, low)

        @pl.when(i == steps - 1)
        def _():
            for q in range(per_row):
                out_ref[:, q * feats:(q + 1) * feats] = up[:, q * fold:(q + 1) * fold].T.astype(BF)
            out_ref[:, per_row * feats:] = jnp.zeros((fold, feats), BF)
            out_ref[:rows, per_row * feats:] = bt[...].astype(BF)

    return pl.pallas_call(
        body,
        out_shape=jax.ShapeDtypeStruct((fold, (per_row + 1) * feats), BF),
        grid=(steps,),
        in_specs=[
            pl.BlockSpec((feats, eb), lambda i: (0, i)),
            pl.BlockSpec((eb, width), lambda i: (i, 0)),
            pl.BlockSpec((per, feats, LO), lambda i: (i, 0, 0)),
            pl.BlockSpec((per, rows, LO), lambda i: (i, 0, 0)),
        ],
        out_specs=full((fold, (per_row + 1) * feats)),
        scratch_shapes=[pltpu.VMEM((feats, width), F32), pltpu.VMEM((rows, feats), F32)],
        compiler_params=params(),
        name="weights",
    )(agg_t, g_pre, g_basis, trip)


def return_kernel(ret, send_idx, edges, small):
    peers, feats, slot = ret.shape
    n_edges, width = edges.shape
    fold = small.shape[0]
    lanes = width // fold * feats + small.shape[1]
    per = 8
    steps = peers // per
    eblocks = n_edges // LO
    eb = 512
    esteps = n_edges // eb

    def body(r_ref, i_ref, e_ref, s_ref, down_out, grad_out, acc, pm, oh, gacc):
        i = pl.program_id(0)

        @pl.when(i == 0)
        def _():
            acc[...] = jnp.zeros_like(acc)
            gacc[...] = jnp.zeros_like(gacc)

        @pl.when(i < steps)
        def _():
            for a in range(per):
                cols = slice(a * slot, (a + 1) * slot)
                lo, hi = split(i_ref[:, cols])
                rows = r_ref[a].astype(F32)
                for j in range(eblocks):
                    pm[j * feats:(j + 1) * feats, cols] = jnp.where(hi == j, rows, 0.0).astype(BF)
                oh[:, cols] = onehot(lo, slot)
            acc[...] += nt(pm[...], oh[...])

        @pl.when(i == steps - 1)
        def _():
            for j in range(eblocks):
                down_out[:, j * LO:(j + 1) * LO] = acc[j * feats:(j + 1) * feats].astype(BF)

        @pl.when(i >= steps)
        def _():
            k = i - steps
            gacc[...] += nn(down_out[:, pl.ds(pl.multiple_of(k * eb, eb), eb)], e_ref[...])

        @pl.when(i == steps + esteps - 1)
        def _():
            for q in range(width // fold):
                grad_out[:, q * feats:(q + 1) * feats] = gacc[:, q * fold:(q + 1) * fold].T.astype(BF)
            grad_out[:, width // fold * feats:] = s_ref[...]

    return pl.pallas_call(
        body,
        out_shape=(
            jax.ShapeDtypeStruct((feats, n_edges), BF),
            jax.ShapeDtypeStruct((fold, lanes), BF),
        ),
        grid=(steps + esteps,),
        in_specs=[
            pl.BlockSpec((per, feats, slot), lambda i: (jnp.minimum(i, steps - 1), 0, 0)),
            pl.BlockSpec((1, per * slot), lambda i: (0, jnp.minimum(i, steps - 1))),
            pl.BlockSpec((eb, width), lambda i: (jnp.maximum(i - steps, 0), 0)),
            full(small.shape),
        ],
        out_specs=(full((feats, n_edges)), full((fold, lanes))),
        scratch_shapes=[
            pltpu.VMEM((eblocks * feats, LO), F32),
            pltpu.VMEM((eblocks * feats, per * slot), BF),
            pltpu.VMEM((LO, per * slot), BF),
            pltpu.VMEM((feats, width), F32),
        ],
        compiler_params=params(),
        name="returned",
    )(ret, send_idx, edges, small)


def edges_kernel(g_down_t, w_down_t):
    feats, n_edges = g_down_t.shape
    width = w_down_t.shape[1]
    eb = 512

    def body(g_ref, w_ref, out_ref):
        out_ref[...] = tn(g_ref[...], w_ref[...]).astype(BF)

    return pl.pallas_call(
        body,
        out_shape=jax.ShapeDtypeStruct((n_edges, width), BF),
        grid=(n_edges // eb,),
        in_specs=[pl.BlockSpec((feats, eb), lambda i: (0, i)), full(w_down_t.shape)],
        out_specs=pl.BlockSpec((eb, width), lambda i: (i, 0)),
        compiler_params=params(),
        name="grad_edges",
    )(g_down_t, w_down_t)


def exchange(x, axes):
    return lax.all_to_all(x, axes, split_axis=0, concat_axis=0, tiled=True)


def reduce_all(x, n):
    rows, width = x.shape
    slab = (rows // n, width)
    mine = exchange(x.reshape((n,) + slab), ("dp", "graph")).astype(F32).sum(axis=0)
    spread = jnp.broadcast_to(mine.astype(BF)[None], (n,) + slab)
    return exchange(spread, ("dp", "graph")).reshape(rows, width)


def make_shards(n_dp, n_graph):
    def shards(edges, send_rows, trip_src, trip_dst, basis_values, cotangent, w_down, w_up, w_basis):
        edge_rows = edges[0]
        basis = basis_values[0]
        n_edges, width = edge_rows.shape
        feats = w_down.shape[1]
        nb = basis.shape[0]
        sent = send_kernel(edge_rows, w_down, send_rows, n_graph)
        received = exchange(sent, "graph")
        src, sent_now = lax.optimization_barrier((trip_src, sent))
        trip, ranges = sort_kernel(src, trip_dst, basis, n_graph)
        w_basis_t = jnp.pad(w_basis.T, ((0, 0), (0, trip.shape[1] - nb)))
        src_t, agg_t = forward_kernel(received, ranges, trip, w_basis_t, n_edges, nb)
        g_pre, g_agg_t = dense_kernel(agg_t, w_up, cotangent[0])
        g_received, g_basis = backward_kernel(
            g_agg_t, src_t, ranges, trip, w_basis_t, n_graph, nb
        )
        returned = exchange(g_received, "graph")
        small = weights_kernel(agg_t, g_pre, g_basis, trip, 2 * n_dp * n_graph)
        g_down_t, terms = return_kernel(returned, send_rows, edge_rows, small)
        reduced = reduce_all(terms, n_dp * n_graph)
        grad_edges = edges_kernel(g_down_t, w_down.T)
        fold = reduced.shape[0]
        parts = [reduced[:, k * feats:(k + 1) * feats] for k in range(reduced.shape[1] // feats)]
        per = width // fold
        grad_down = jnp.concatenate(parts[:per]).astype(F32)
        grad_up = jnp.concatenate(parts[per:2 * per]).astype(F32).T
        grad_basis = parts[2 * per][:nb].astype(F32)
        return grad_edges[None], grad_down, grad_up, grad_basis

    return shards


def solution(mesh):
    shape = dict(mesh.shape)
    in_specs = (
        P("dp", "graph", None),
        P("dp", "graph"),
        P("dp", "graph"),
        P("dp", "graph"),
        P("dp", None, "graph"),
        P("dp", "graph", None),
        P(),
        P(),
        P(),
    )
    out_specs = (P("dp", "graph", None), P(), P(), P())
    return jax.shard_map(
        make_shards(shape["dp"], shape["graph"]),
        mesh=mesh,
        in_specs=in_specs,
        out_specs=out_specs,
        check_vma=False,
    )
```

time: 309 us -> 250 us (0.81)
  waiting for transfers between devices: 151 us -> 95 us
  blocking collectives: 0 us -> 34.9 us
  starting transfers between devices: 46.7 us -> 24.8 us
  Pallas kernels: 101 us -> 82.5 us
    all_to_all x6 -> x3, waiting for transfers between devices: 151 us -> 95 us  [exchange(): return lax.all_to_all(x, axes, split_axis=0, concat_axis=0, tiled=True)]
    all_to_all x0 -> x1, blocking collectives: none -> 34.9 us  [exchange(): return lax.all_to_all(x, axes, split_axis=0, concat_axis=0, tiled=True)]
    all_to_all x6 -> x3, starting transfers between devices: 46.7 us -> 24.8 us  [exchange(): return lax.all_to_all(x, axes, split_axis=0, concat_axis=0, tiled=True)]
    pallas_call x1, Pallas kernels: 33.6 us -> 14.2 us  [backward_kernel(): pl.pallas_call(body, out_shape=(jax.ShapeDtypeStruct((peers, feats, LO),...]
    pallas_call x2 -> x4, Pallas kernels: 40.4 us -> 41.3 us  [the longest x1 13.7 us: sort_kernel(): pl.pallas_call(body, out_shape=(jax.ShapeDtypeStruct((chunks, rows, LO),...]
  transfers between devices with their start and end apart: 6 -> 3, of which waited for: 6 -> 3; matrix products, arithmetic and copies ran while one was open for 2% -> 1% of each run, Pallas kernels for 5% -> 10%
where the time goes in v2:
time: 250 us; the launch traced here: 249 us
  waiting for transfers between devices  95 us (38%)
  Pallas kernels  82.5 us (33%)
  blocking collectives  34.9 us (14%)
  starting transfers between devices  24.8 us (10%)
  local copies, waits for them, and re-layouts  8.75 us (4%)
    all_to_all x3, waiting for transfers between devices, exchange(): return lax.all_to_all(x, axes, split_axis=0, concat_axis=0, tiled=True)  95 us
    all_to_all x1, blocking collectives, exchange(): return lax.all_to_all(x, axes, split_axis=0, concat_axis=0, tiled=True)  34.9 us
    all_to_all x3, starting transfers between devices, exchange(): return lax.all_to_all(x, axes, split_axis=0, concat_axis=0, tiled=True)  24.8 us
    pallas_call x1, Pallas kernels, backward_kernel(): pl.pallas_call(body, out_shape=(jax.ShapeDtypeStruct((peers, feats, LO),...  14.2 us
    pallas_call x1, Pallas kernels, sort_kernel(): pl.pallas_call(body, out_shape=(jax.ShapeDtypeStruct((chunks, rows, LO),...  13.7 us
    pallas_call x1, Pallas kernels, forward_kernel(): pl.pallas_call(body, out_shape=(jax.ShapeDtypeStruct((chunks, feats, LO),...  11.9 us
    pallas_call x1, Pallas kernels, return_kernel(): pl.pallas_call(body, out_shape=(jax.ShapeDtypeStruct((feats, n_edges), BF...  11.3 us
    pallas_call x1, Pallas kernels, send_kernel(): pl.pallas_call(body, out_shape=jax.ShapeDtypeStruct((peers, feats, slot),...  10.9 us
  transfers between devices with their start and end apart: 3, of which 3 were waited for; matrix products, arithmetic and copies ran while one was open for 1% of the time, Pallas kernels for 10%

profile of v2, /device:TPU:1, one launch (start us, length us, event | category | flops | bytes accessed | tf_op | source)
XLA Modules:
  0.0 248.8 jit_solution(1075275260825043216)
XLA Ops:
  0.6 10.9 %send.1 = bf16[32,128,256]{2,1,0:T(8,128)(2,1)} custom-call(bf16[2048,1024]{1,0:T(8,128)(2,1)} %bitcast.8, bf16[1024,128]{1,0:T(8,128)(2,1)} %w_ref.2, s32[1,8192]{1,0:T(1,128)} %i_ref.3), custom_call_target="tpu_custom_call" | custom-call | tf_op jit(solution)/shard_map/send/pallas_call | solution.py:76
  11.6 12.2 %all-to-all-start = ((bf16[32,128,256]{2,1,0:T(8,128)(2,1)}), bf16[32,128,256]{2,1,0:T(8,128)(2,1)S(1)}, u32[]{:S(2)}, u32[]{:S(2)}) async-start(bf16[32,128,256]{2,1,0:T(8,128)(2,1)} %send.1), calls=%async_computation | async-start | bytes 4194304 | tf_op jit(solution)/shard_map/all_to_all | solution.py:516
  23.9 0.6 pad.4.w_ref
  24.5 13.7 %order.1 = (f32[32,48,256]{2,1,0:T(8,128)}, s32[2,128]{1,0:T(2,128)}) custom-call(s32[1,8192]{1,0:T(1,128)} %s_ref, s32[1,8192]{1,0:T(1,128)} %d_ref.1, bf16[42,8192]{1,0:T(8,128)(2,1)} %bitcast.13), custom_call_target="tpu_custom_call" | custom-call | tf_op jit(solution)/shard_map/order/pallas_call | solution.py:150
  38.2 34.4 %all-to-all-done.r_ref = bf16[32,128,256]{2,1,0:T(8,128)(2,1)S(1)} async-done(((bf16[32,128,256]{2,1,0:T(8,128)(2,1)}), bf16[32,128,256]{2,1,0:T(8,128)(2,1)S(1)}, u32[]{:S(2)}, u32[]{:S(2)}) %all-to-all-start) | async-done | bytes 2097184 | tf_op jit(solution)/shard_map/all_to_all | solution.py:516
  72.6 1.3 copy-done.1
  73.9 11.9 %forward.1 = (bf16[32,128,256]{2,1,0:T(8,128)(2,1)}, bf16[128,2048]{1,0:T(8,128)(2,1)}) custom-call(s32[2,128]{1,0:T(2,128)} %get-tuple-element.16.rg, bf16[32,128,256]{2,1,0:T(8,128)(2,1)} %copy-done.1, f32[32,48,256]{2,1,0:T(8,128)} %get-tuple-element.17.x_ref, bf16[128,48]{1,0:T(8,128)(2,1)} %pad.4.w_ref), custom_call_target="tpu_custom_call" | custom-call | tf_op jit(solution)/shard_map/forward/pallas_call | solution.py:234
  85.8 9.3 %dense.1 = (bf16[2048,1024]{1,0:T(8,128)(2,1)}, bf16[128,2048]{1,0:T(8,128)(2,1)}) custom-call(bf16[128,2048]{1,0:T(8,128)(2,1)} %get-tuple-element.18.a_ref, bf16[128,1024]{1,0:T(8,128)(2,1)} %w_ref.3, bf16[2048,1024]{1,0:T(8,128)(2,1)} %bitcast.10), custom_call_target="tpu_custom_call" | custom-call | tf_op jit(solution)/shard_map/dense/pallas_call | solution.py:277
  95.1 14.2 %backward.1 = (bf16[32,128,256]{2,1,0:T(8,128)(2,1)}, f32[32,128,256]{2,1,0:T(8,128)}) custom-call(s32[2,128]{1,0:T(2,128)} %get-tuple-element.16.rg, bf16[128,2048]{1,0:T(8,128)(2,1)} %get-tuple-element.19.g_ref, bf16[32,128,256]{2,1,0:T(8,128)(2,1)} %get-tuple-element.20.st_ref, f32[32,48,256]{2,1,0:T(8,128)} %get-tuple-element.17.x_ref, ...), custom_call_target="tpu_custom_call" | custom-call | tf_op jit(solution)/shard_map/backward/pallas_call | solution.py:347
  109.3 7.2 %all-to-all-start.1 = ((bf16[32,128,256]{2,1,0:T(8,128)(2,1)}), bf16[32,128,256]{2,1,0:T(8,128)(2,1)S(1)}, u32[]{:S(2)}, u32[]{:S(2)}) async-start(bf16[32,128,256]{2,1,0:T(8,128)(2,1)} %get-tuple-element.21), calls=%async_computation.1 | async-start | bytes 4194304 | tf_op jit(solution)/shard_map/all_to_all | solution.py:516
  116.5 6.4 %weights.1.s_ref = bf16[512,384]{1,0:T(8,128)(2,1)} custom-call(bf16[128,2048]{1,0:T(8,128)(2,1)} %get-tuple-element.18.a_ref, bf16[2048,1024]{1,0:T(8,128)(2,1)} %get-tuple-element.22.p_ref, f32[32,128,256]{2,1,0:T(8,128)} %get-tuple-element.23.g_ref, f32[32,48,256]{2,1,0:T(8,128)} %get-tuple-element.17.x_ref), custom_call_target="tpu_custom_call" | custom-call | tf_op jit(solution)/shard_map/weights/pallas_call | solution.py:408
  122.9 42.1 %all-to-all-done.1.r_ref = bf16[32,128,256]{2,1,0:T(8,128)(2,1)S(1)} async-done(((bf16[32,128,256]{2,1,0:T(8,128)(2,1)}), bf16[32,128,256]{2,1,0:T(8,128)(2,1)S(1)}, u32[]{:S(2)}, u32[]{:S(2)}) %all-to-all-start.1) | async-done | bytes 2097184 | tf_op jit(solution)/shard_map/all_to_all | solution.py:516
  165.0 1.3 copy-done
  166.3 11.3 %returned.1 = (bf16[128,2048]{1,0:T(8,128)(2,1)}, bf16[512,640]{1,0:T(8,128)(2,1)}) custom-call(bf16[32,128,256]{2,1,0:T(8,128)(2,1)} %copy-done, s32[1,8192]{1,0:T(1,128)} %i_ref.3, bf16[2048,1024]{1,0:T(8,128)(2,1)} %bitcast.9, bf16[512,384]{1,0:T(8,128)(2,1)} %weights.1.s_ref), custom_call_target="tpu_custom_call" | custom-call | tf_op jit(solution)/shard_map/returned/pallas_call | solution.py:471
  177.7 2.0 reshape.15
  179.7 34.9 %all_to_all.20 = bf16[256,2,640]{2,1,0:T(2,128)(2,1)S(1)} all-to-all(bf16[256,2,640]{2,1,0:T(2,128)(2,1)S(1)} %reshape.15), channel_id=1, replica_groups=mesh['dp'=8,'graph'=32] {'dp','graph'}, dimensions={0} | all-to-all | bytes 1310720 | tf_op jit(solution)/shard_map/all_to_all | solution.py:516
  215.2 1.2 broadcast_in_dim.10
  216.4 5.4 %all-to-all-start.3 = ((bf16[256,2,640]{2,1,0:T(2,128)(2,1)}), bf16[256,2,640]{2,1,0:T(2,128)(2,1)S(1)}, u32[]{:S(2)}, u32[]{:S(2)}) async-start(bf16[256,2,640]{2,1,0:T(2,128)(2,1)} %broadcast_in_dim.10), calls=%async_computation.3 | async-start | bytes 1310720 | tf_op jit(solution)/shard_map/all_to_all | solution.py:516
  221.8 0.9 copy.14
  222.7 4.8 %grad_edges.1 = bf16[2048,1024]{1,0:T(8,128)(2,1)} custom-call(bf16[128,2048]{1,0:T(8,128)(2,1)} %get-tuple-element.24.g_ref, bf16[128,1024]{1,0:T(8,128)(2,1)} %bitcast.12), custom_call_target="tpu_custom_call" | custom-call | tf_op jit(solution)/shard_map/grad_edges/pallas_call | solution.py:504
  227.5 18.5 %all-to-all-done.3 = bf16[256,2,640]{2,1,0:T(2,128)(2,1)S(1)} async-done(((bf16[256,2,640]{2,1,0:T(2,128)(2,1)}), bf16[256,2,640]{2,1,0:T(2,128)(2,1)S(1)}, u32[]{:S(2)}, u32[]{:S(2)}) %all-to-all-start.3) | async-done | bytes 655392 | tf_op jit(solution)/shard_map/all_to_all | solution.py:516
  246.3 0.6 slice_convert_fusion
  246.9 0.9 convert_bitcast_fusion
  247.8 1.0 copy.15
  (10 shorter events, 1.1 us)
Async XLA Ops:
  11.6 12.2 %copy-start.3 = (bf16[42,128]{1,0:T(8,128)(2,1)S(1)}, bf16[42,128]{1,0:T(8,128)(2,1)}, u32[]{:S(2)}) copy-start(bf16[42,128]{1,0:T(8,128)(2,1)} %param.17) | copy-start | bytes 32260
  11.6 61.0 %all-to-all-start = ((bf16[32,128,256]{2,1,0:T(8,128)(2,1)}), bf16[32,128,256]{2,1,0:T(8,128)(2,1)S(1)}, u32[]{:S(2)}, u32[]{:S(2)}) async-start(bf16[32,128,256]{2,1,0:T(8,128)(2,1)} %send.1), calls=%async_computation | async-start | bytes 4194304 | tf_op jit(solution)/shard_map/all_to_all | solution.py:516
  72.6 1.3 copy-start.1
  109.3 55.7 %all-to-all-start.1 = ((bf16[32,128,256]{2,1,0:T(8,128)(2,1)}), bf16[32,128,256]{2,1,0:T(8,128)(2,1)S(1)}, u32[]{:S(2)}, u32[]{:S(2)}) async-start(bf16[32,128,256]{2,1,0:T(8,128)(2,1)} %get-tuple-element.21), calls=%async_computation.1 | async-start | bytes 4194304 | tf_op jit(solution)/shard_map/all_to_all | solution.py:516
  165.0 1.3 copy-start
  179.7 42.2 %copy-start.2 = (bf16[1024,128]{1,0:T(8,128)(2,1)S(1)}, bf16[1024,128]{1,0:T(8,128)(2,1)}, u32[]{:S(2)}) copy-start(bf16[1024,128]{1,0:T(8,128)(2,1)} %w_ref.2) | copy-start | bytes 786436
  216.4 29.5 %all-to-all-start.3 = ((bf16[256,2,640]{2,1,0:T(2,128)(2,1)}), bf16[256,2,640]{2,1,0:T(2,128)(2,1)S(1)}, u32[]{:S(2)}, u32[]{:S(2)}) async-start(bf16[256,2,640]{2,1,0:T(2,128)(2,1)} %broadcast_in_dim.10), calls=%async_computation.3 | async-start | bytes 1310720 | tf_op jit(solution)/shard_map/all_to_all | solution.py:516

commit v3 on v2

--- a/solution.py
+++ b/solution.py
@@ -49,9 +49,9 @@
 def send_kernel(edges, w_down, send_idx, peers):
     n_edges, width = edges.shape
     feats = w_down.shape[1]
-    eb = 512
+    eb = 1024
     nd = n_edges // eb
-    per = 4
+    per = 16
     ng = peers // per
     slot = send_idx.shape[1] // peers
     blocks = n_edges // LO
@@ -178,7 +178,7 @@
 def forward_kernel(recv, ranges, trip, w_basis_t, n_edges, nb):
     peers, feats, _ = recv.shape
     chunks, rows, _ = trip.shape
-    per = 8
+    per = 16
     steps = chunks // per
     eblocks = n_edges // LO
 
@@ -264,15 +264,17 @@
 def dense_kernel(agg_t, w_up, cot):
     feats, n_edges = agg_t.shape
     width = w_up.shape[1]
-    eb = 256
+    eb = 1024
     steps = n_edges // eb
 
     def body(a_ref, w_ref, c_ref, p_out, g_out):
-        pre = tn(a_ref[...], w_ref[...])
-        t = 0.5 * jnp.tanh(0.5 * pre)
-        g_pre = (c_ref[...].astype(F32) * (0.5 + t) * (1.0 + pre * (0.5 - t))).astype(BF)
-        p_out[...] = g_pre
-        g_out[...] = nt(w_ref[...], g_pre).astype(BF)
+        for k in range(eb // 256):
+            r = slice(k * 256, (k + 1) * 256)
+            pre = tn(a_ref[:, r], w_ref[...])
+            t = 0.5 * jnp.tanh(0.5 * pre)
+            g_pre = (c_ref[r].astype(F32) * (0.5 + t) * (1.0 + pre * (0.5 - t))).astype(BF)
+            p_out[r] = g_pre
+            g_out[:, r] = nt(w_ref[...], g_pre).astype(BF)
 
     return pl.pallas_call(
         body,
@@ -374,14 +376,13 @@
     )(ranges, g_agg_t, src_t, trip, w_basis_t)
 
 
-def weights_kernel(agg_t, g_pre, g_basis, trip, fold):
+def weights_kernel(agg_t, g_pre, g_basis, trip, lines):
     feats, n_edges = agg_t.shape
     width = g_pre.shape[1]
     chunks, rows, _ = trip.shape
     steps = 4
     eb = n_edges // steps
     per = chunks // steps
-    per_row = width // fold
 
     def body(a_ref, p_ref, g_ref, x_ref, out_ref, up, bt):
         i = pl.program_id(0)
@@ -400,14 +401,13 @@
 
         @pl.when(i == steps - 1)
         def _():
-            for q in range(per_row):
-                out_ref[:, q * feats:(q + 1) * feats] = up[:, q * fold:(q + 1) * fold].T.astype(BF)
-            out_ref[:, per_row * feats:] = jnp.zeros((fold, feats), BF)
-            out_ref[:rows, per_row * feats:] = bt[...].astype(BF)
-
-    return pl.pallas_call(
-        body,
-        out_shape=jax.ShapeDtypeStruct((fold, (per_row + 1) * feats), BF),
+            out_ref[:, :width] = up[...]
+            tall = jnp.concatenate([bt[...], jnp.zeros((lines - rows, feats), F32)])
+            out_ref[:, width:] = tall.T
+
+    return pl.pallas_call(
+        body,
+        out_shape=jax.ShapeDtypeStruct((feats, width + lines), F32),
         grid=(steps,),
         in_specs=[
             pl.BlockSpec((feats, eb), lambda i: (0, i)),
@@ -415,25 +415,25 @@
             pl.BlockSpec((per, feats, LO), lambda i: (i, 0, 0)),
             pl.BlockSpec((per, rows, LO), lambda i: (i, 0, 0)),
         ],
-        out_specs=full((fold, (per_row + 1) * feats)),
+        out_specs=full((feats, width + lines)),
         scratch_shapes=[pltpu.VMEM((feats, width), F32), pltpu.VMEM((rows, feats), F32)],
         compiler_params=params(),
         name="weights",
     )(agg_t, g_pre, g_basis, trip)
 
 
-def return_kernel(ret, send_idx, edges, small):
+def return_kernel(ret, send_idx, edges, piece):
     peers, feats, slot = ret.shape
     n_edges, width = edges.shape
-    fold = small.shape[0]
-    lanes = width // fold * feats + small.shape[1]
-    per = 8
+    fold = piece.shape[0]
+    lanes = width // fold * feats + piece.shape[1]
+    per = 32
     steps = peers // per
     eblocks = n_edges // LO
-    eb = 512
+    eb = 2048
     esteps = n_edges // eb
 
-    def body(r_ref, i_ref, e_ref, s_ref, down_out, grad_out, acc, pm, oh, gacc):
+    def body(r_ref, i_ref, e_ref, p_ref, down_out, grad_out, acc, pm, oh, gacc):
         i = pl.program_id(0)
 
         @pl.when(i == 0)
@@ -466,7 +466,7 @@
         def _():
             for q in range(width // fold):
                 grad_out[:, q * feats:(q + 1) * feats] = gacc[:, q * fold:(q + 1) * fold].T.astype(BF)
-            grad_out[:, width // fold * feats:] = s_ref[...]
+            grad_out[:, width // fold * feats:] = p_ref[...]
 
     return pl.pallas_call(
         body,
@@ -479,7 +479,7 @@
             pl.BlockSpec((per, feats, slot), lambda i: (jnp.minimum(i, steps - 1), 0, 0)),
             pl.BlockSpec((1, per * slot), lambda i: (0, jnp.minimum(i, steps - 1))),
             pl.BlockSpec((eb, width), lambda i: (jnp.maximum(i - steps, 0), 0)),
-            full(small.shape),
+            full(piece.shape),
         ],
         out_specs=(full((feats, n_edges)), full((fold, lanes))),
         scratch_shapes=[
@@ -490,13 +490,13 @@
         ],
         compiler_params=params(),
         name="returned",
-    )(ret, send_idx, edges, small)
+    )(ret, send_idx, edges, piece)
 
 
 def edges_kernel(g_down_t, w_down_t):
     feats, n_edges = g_down_t.shape
     width = w_down_t.shape[1]
-    eb = 512
+    eb = 1024
 
     def body(g_ref, w_ref, out_ref):
         out_ref[...] = tn(g_ref[...], w_ref[...]).astype(BF)
@@ -516,12 +516,45 @@
     return lax.all_to_all(x, axes, split_axis=0, concat_axis=0, tiled=True)
 
 
-def reduce_all(x, n):
-    rows, width = x.shape
-    slab = (rows // n, width)
-    mine = exchange(x.reshape((n,) + slab), ("dp", "graph")).astype(F32).sum(axis=0)
-    spread = jnp.broadcast_to(mine.astype(BF)[None], (n,) + slab)
-    return exchange(spread, ("dp", "graph")).reshape(rows, width)
+def total_kernel(got, n_dp, feats, own):
+    n, pair, lanes = got.shape
+    share = feats // n_dp
+    groups = (lanes - own) // feats * 3
+    out_lanes = own + groups * feats
+
+    def body(x_ref, out_ref):
+        sums = jnp.sum(x_ref[...].astype(F32).reshape(n_dp, n // n_dp, pair, lanes), axis=1)
+        parts = [jnp.sum(sums[:, :, :own], axis=0)]
+        where = lax.broadcasted_iota(jnp.int32, (n_dp, pair, feats), 2) // share
+        mine = where == lax.broadcasted_iota(jnp.int32, (n_dp, pair, feats), 0)
+        for q in range(groups):
+            piece = sums[:, :, own + q * share:own + (q + 1) * share]
+            wide = jnp.concatenate([piece] * n_dp, axis=2)
+            parts.append(jnp.sum(jnp.where(mine, wide, 0.0), axis=0))
+        row = jnp.concatenate(parts, axis=1).astype(BF)
+        out_ref[...] = jnp.broadcast_to(row[None], out_ref.shape)
+
+    return pl.pallas_call(
+        body,
+        out_shape=jax.ShapeDtypeStruct((n, pair, out_lanes), BF),
+        compiler_params=params(),
+        name="totals",
+    )(got)
+
+
+def share_out(part, fold):
+    share, cols = part.shape
+    tall = jnp.pad(part.T.astype(BF), ((0, -cols % fold), (0, 0)))
+    wide = jnp.concatenate([tall[k:k + fold] for k in range(0, tall.shape[0], fold)], axis=1)
+    return jnp.pad(wide, ((0, 0), (0, -wide.shape[1] % 128)))
+
+
+def reduce_all(slab, n_dp, n_graph, feats, own):
+    n = n_dp * n_graph
+    axes = ("dp", "graph")
+    got = exchange(slab.reshape(n, slab.shape[0] // n, slab.shape[1]), axes)
+    sent = total_kernel(got, n_dp, feats, own)
+    return exchange(sent, axes).reshape(slab.shape[0], sent.shape[2])
 
 
 def make_shards(n_dp, n_graph):
@@ -542,11 +575,14 @@
             g_agg_t, src_t, ranges, trip, w_basis_t, n_graph, nb
         )
         returned = exchange(g_received, "graph")
-        small = weights_kernel(agg_t, g_pre, g_basis, trip, 2 * n_dp * n_graph)
-        g_down_t, terms = return_kernel(returned, send_rows, edge_rows, small)
-        reduced = reduce_all(terms, n_dp * n_graph)
+        n = n_dp * n_graph
+        fold = 2 * n
+        small = weights_kernel(agg_t, g_pre, g_basis, trip, n)
+        part = lax.psum_scatter(small, "dp", scatter_dimension=0, tiled=True)
+        returned, piece = lax.optimization_barrier((returned, share_out(part, fold)))
+        g_down_t, slab = return_kernel(returned, send_rows, edge_rows, piece)
+        reduced = reduce_all(slab, n_dp, n_graph, feats, width // fold * feats)
         grad_edges = edges_kernel(g_down_t, w_down.T)
-        fold = reduced.shape[0]
         parts = [reduced[:, k * feats:(k + 1) * feats] for k in range(reduced.shape[1] // feats)]
         per = width // fold
         grad_down = jnp.concatenate(parts[:per]).astype(F32)

time: 250 us -> 250 us (level)
  between operations: 0.71 us -> 14.1 us
  blocking collectives: 34.9 us -> 29.4 us
  Pallas kernels: 82.5 us -> 77.3 us
    all_to_all x3, waiting for transfers between devices: 95 us -> 59.7 us  [exchange(): return lax.all_to_all(x, axes, split_axis=0, concat_axis=0, tiled=True)]
    unnamed x0 -> x2, waiting for transfers between devices: none -> 34 us
    all_to_all x1, blocking collectives: 34.9 us -> 29.4 us  [exchange(): return lax.all_to_all(x, axes, split_axis=0, concat_axis=0, tiled=True)]
    pallas_call x1 -> x2, Pallas kernels: 6.37 us -> 8.82 us  [the longest x1 6.46 us: weights_kernel(): pl.pallas_call(body, out_shape=jax.ShapeDtypeStruct((feats, width + lines...]
    unnamed x11 -> x12, local copies, waits for them, and re-layouts: 4.62 us -> 5.72 us
  transfers between devices with their start and end apart: 3 -> 4, of which waited for: 3 -> 4; matrix products, arithmetic and copies ran while one was open for 1% -> 1% of each run, Pallas kernels for 10% -> 10%
where the time goes in v3:
time: 250 us
  waiting for transfers between devices  93.6 us (37%)
  Pallas kernels  77.3 us (31%)
  blocking collectives  29.4 us (12%)
  starting transfers between devices  25.1 us (10%)
  between operations  14.1 us (6%)
  local copies, waits for them, and re-layouts  7.9 us (3%)
    all_to_all x3, waiting for transfers between devices, exchange(): return lax.all_to_all(x, axes, split_axis=0, concat_axis=0, tiled=True)  59.7 us
    unnamed x2, waiting for transfers between devices  34 us
    all_to_all x1, blocking collectives, exchange(): return lax.all_to_all(x, axes, split_axis=0, concat_axis=0, tiled=True)  29.4 us
    all_to_all x3, starting transfers between devices, exchange(): return lax.all_to_all(x, axes, split_axis=0, concat_axis=0, tiled=True)  24.8 us
    pallas_call x1, Pallas kernels, backward_kernel(): pl.pallas_call(body, out_shape=(jax.ShapeDtypeStruct((peers, feats, LO),...  14.2 us
    pallas_call x1, Pallas kernels, sort_kernel(): pl.pallas_call(body, out_shape=(jax.ShapeDtypeStruct((chunks, rows, LO),...  13.7 us
    pallas_call x1, Pallas kernels, forward_kernel(): pl.pallas_call(body, out_shape=(jax.ShapeDtypeStruct((chunks, feats, LO),...  11.3 us
    pallas_call x1, Pallas kernels, return_kernel(): pl.pallas_call(body, out_shape=(jax.ShapeDtypeStruct((feats, n_edges), BF...  9.37 us
  transfers between devices with their start and end apart: 4, of which 4 were waited for; matrix products, arithmetic and copies ran while one was open for 1% of the time, Pallas kernels for 10%

profile of v3, /device:TPU:1, one launch (start us, length us, event | category | flops | bytes accessed | tf_op | source)
XLA Modules:
  0.0 249.7 jit_solution(3921146268870920125)
XLA Ops:
  7.2 9.0 %send.1 = bf16[32,128,256]{2,1,0:T(8,128)(2,1)} custom-call(bf16[2048,1024]{1,0:T(8,128)(2,1)} %bitcast.12, bf16[1024,128]{1,0:T(8,128)(2,1)} %w_ref.2, s32[1,8192]{1,0:T(1,128)} %i_ref.3), custom_call_target="tpu_custom_call" | custom-call | tf_op jit(solution)/shard_map/send/pallas_call | solution.py:76
  16.2 12.3 %all-to-all-start = ((bf16[32,128,256]{2,1,0:T(8,128)(2,1)}), bf16[32,128,256]{2,1,0:T(8,128)(2,1)S(1)}, u32[]{:S(2)}, u32[]{:S(2)}) async-start(bf16[32,128,256]{2,1,0:T(8,128)(2,1)} %send.1), calls=%async_computation | async-start | bytes 4194304 | tf_op jit(solution)/shard_map/all_to_all | solution.py:516
  29.3 13.7 %order.1 = (f32[32,48,256]{2,1,0:T(8,128)}, s32[2,128]{1,0:T(2,128)}) custom-call(s32[1,8192]{1,0:T(1,128)} %s_ref, s32[1,8192]{1,0:T(1,128)} %d_ref.1, bf16[42,8192]{1,0:T(8,128)(2,1)} %bitcast.18), custom_call_target="tpu_custom_call" | custom-call | tf_op jit(solution)/shard_map/order/pallas_call | solution.py:150
  43.0 34.2 %all-to-all-done.r_ref = bf16[32,128,256]{2,1,0:T(8,128)(2,1)S(1)} async-done(((bf16[32,128,256]{2,1,0:T(8,128)(2,1)}), bf16[32,128,256]{2,1,0:T(8,128)(2,1)S(1)}, u32[]{:S(2)}, u32[]{:S(2)}) %all-to-all-start) | async-done | bytes 2097184 | tf_op jit(solution)/shard_map/all_to_all | solution.py:516
  77.2 1.3 copy-done.1
  78.5 11.3 %forward.1 = (bf16[32,128,256]{2,1,0:T(8,128)(2,1)}, bf16[128,2048]{1,0:T(8,128)(2,1)}) custom-call(s32[2,128]{1,0:T(2,128)} %get-tuple-element.18.rg, bf16[32,128,256]{2,1,0:T(8,128)(2,1)} %copy-done.1, f32[32,48,256]{2,1,0:T(8,128)} %get-tuple-element.19.x_ref, bf16[128,48]{1,0:T(8,128)(2,1)} %pad.12.w_ref), custom_call_target="tpu_custom_call" | custom-call | tf_op jit(solution)/shard_map/forward/pallas_call | solution.py:234
  89.8 7.1 %dense.1 = (bf16[2048,1024]{1,0:T(8,128)(2,1)}, bf16[128,2048]{1,0:T(8,128)(2,1)}) custom-call(bf16[128,2048]{1,0:T(8,128)(2,1)} %get-tuple-element.20.a_ref, bf16[128,1024]{1,0:T(8,128)(2,1)} %w_ref.3, bf16[2048,1024]{1,0:T(8,128)(2,1)} %bitcast.14), custom_call_target="tpu_custom_call" | custom-call | tf_op jit(solution)/shard_map/dense/pallas_call | solution.py:279
  96.9 14.2 %backward.1 = (bf16[32,128,256]{2,1,0:T(8,128)(2,1)}, f32[32,128,256]{2,1,0:T(8,128)}) custom-call(s32[2,128]{1,0:T(2,128)} %get-tuple-element.18.rg, bf16[128,2048]{1,0:T(8,128)(2,1)} %get-tuple-element.21.g_ref, bf16[32,128,256]{2,1,0:T(8,128)(2,1)} %get-tuple-element.22.st_ref, f32[32,48,256]{2,1,0:T(8,128)} %get-tuple-element.19.x_ref, ...), custom_call_target="tpu_custom_call" | custom-call | tf_op jit(solution)/shard_map/backward/pallas_call | solution.py:349
  111.1 7.0 %all-to-all-start.1 = ((bf16[32,128,256]{2,1,0:T(8,128)(2,1)}), bf16[32,128,256]{2,1,0:T(8,128)(2,1)S(1)}, u32[]{:S(2)}, u32[]{:S(2)}) async-start(bf16[32,128,256]{2,1,0:T(8,128)(2,1)} %get-tuple-element.23), calls=%async_computation.1 | async-start | bytes 4194304 | tf_op jit(solution)/shard_map/all_to_all | solution.py:516
  118.4 6.5 %weights.1 = f32[128,1280]{1,0:T(8,128)} custom-call(bf16[128,2048]{1,0:T(8,128)(2,1)} %get-tuple-element.20.a_ref, bf16[2048,1024]{1,0:T(8,128)(2,1)} %get-tuple-element.24.p_ref, f32[32,128,256]{2,1,0:T(8,128)} %get-tuple-element.25.g_ref, f32[32,48,256]{2,1,0:T(8,128)} %get-tuple-element.19.x_ref), custom_call_target="tpu_custom_call" | custom-call | tf_op jit(solution)/shard_map/weights/pallas_call | solution.py:408
  124.9 33.9 %reduce-scatter.4.cloned.1.call-done = f32[16,1280]{1,0:T(8,128)} async-done(((f32[128,1280]{1,0:T(8,128)}), f32[16,1280]{1,0:T(8,128)}) %reduce-scatter.4.cloned.1.call-update) | async-done | bytes 81936
  158.8 1.1 copy.30
  160.8 6.0 %all-to-all-done.1.r_ref = bf16[32,128,256]{2,1,0:T(8,128)(2,1)S(1)} async-done(((bf16[32,128,256]{2,1,0:T(8,128)(2,1)}), bf16[32,128,256]{2,1,0:T(8,128)(2,1)S(1)}, u32[]{:S(2)}, u32[]{:S(2)}) %all-to-all-start.1) | async-done | bytes 2097184 | tf_op jit(solution)/shard_map/all_to_all | solution.py:516
  166.8 1.3 copy-done
  168.1 9.4 %returned.1 = (bf16[128,2048]{1,0:T(8,128)(2,1)}, bf16[512,384]{1,0:T(8,128)(2,1)}) custom-call(bf16[32,128,256]{2,1,0:T(8,128)(2,1)} %copy-done, s32[1,8192]{1,0:T(1,128)} %i_ref.3, bf16[2048,1024]{1,0:T(8,128)(2,1)} %bitcast.13, bf16[512,128]{1,0:T(8,128)(2,1)} %fusion.4.p_ref), custom_call_target="tpu_custom_call" | custom-call | tf_op jit(solution)/shard_map/returned/pallas_call | solution.py:471
  177.5 1.2 reshape.14
  178.7 29.4 %all_to_all.20.x_ref = bf16[256,2,384]{2,1,0:T(2,128)(2,1)} all-to-all(bf16[256,2,384]{2,1,0:T(2,128)(2,1)S(1)} %reshape.14), channel_id=1, replica_groups=mesh['dp'=8,'graph'=32] {'dp','graph'}, dimensions={0} | all-to-all | bytes 786432 | tf_op jit(solution)/shard_map/all_to_all | solution.py:516
  208.1 2.4 totals.1
  210.5 5.5 %all-to-all-start.3 = ((bf16[256,2,640]{2,1,0:T(2,128)(2,1)}), bf16[256,2,640]{2,1,0:T(2,128)(2,1)S(1)}, u32[]{:S(2)}, u32[]{:S(2)}) async-start(bf16[256,2,640]{2,1,0:T(2,128)(2,1)} %totals.1), calls=%async_computation.3 | async-start | bytes 1310720 | tf_op jit(solution)/shard_map/all_to_all | solution.py:516
  216.0 0.9 copy.27
  216.8 3.8 %grad_edges.1 = bf16[2048,1024]{1,0:T(8,128)(2,1)} custom-call(bf16[128,2048]{1,0:T(8,128)(2,1)} %get-tuple-element.28.g_ref, bf16[128,1024]{1,0:T(8,128)(2,1)} %bitcast.17), custom_call_target="tpu_custom_call" | custom-call | tf_op jit(solution)/shard_map/grad_edges/pallas_call | solution.py:504
  220.6 19.4 %all-to-all-done.3 = bf16[256,2,640]{2,1,0:T(2,128)(2,1)S(1)} async-done(((bf16[256,2,640]{2,1,0:T(2,128)(2,1)}), bf16[256,2,640]{2,1,0:T(2,128)(2,1)S(1)}, u32[]{:S(2)}, u32[]{:S(2)}) %all-to-all-start.3) | async-done | bytes 655392 | tf_op jit(solution)/shard_map/all_to_all | solution.py:516
  241.0 0.9 convert_bitcast_fusion
  241.9 1.0 copy.28
  (15 shorter events, 2.8 us)
Async XLA Ops:
  16.2 12.4 %copy-start.3 = (bf16[42,128]{1,0:T(8,128)(2,1)S(1)}, bf16[42,128]{1,0:T(8,128)(2,1)}, u32[]{:S(2)}) copy-start(bf16[42,128]{1,0:T(8,128)(2,1)} %param.17) | copy-start | bytes 32260
  16.2 61.0 %all-to-all-start = ((bf16[32,128,256]{2,1,0:T(8,128)(2,1)}), bf16[32,128,256]{2,1,0:T(8,128)(2,1)S(1)}, u32[]{:S(2)}, u32[]{:S(2)}) async-start(bf16[32,128,256]{2,1,0:T(8,128)(2,1)} %send.1), calls=%async_computation | async-start | bytes 4194304 | tf_op jit(solution)/shard_map/all_to_all | solution.py:516
  77.2 1.3 copy-start.1
  111.1 55.7 %all-to-all-start.1 = ((bf16[32,128,256]{2,1,0:T(8,128)(2,1)}), bf16[32,128,256]{2,1,0:T(8,128)(2,1)S(1)}, u32[]{:S(2)}, u32[]{:S(2)}) async-start(bf16[32,128,256]{2,1,0:T(8,128)(2,1)} %get-tuple-element.23), calls=%async_computation.1 | async-start | bytes 4194304 | tf_op jit(solution)/shard_map/all_to_all | solution.py:516
  118.1 40.7 %reduce-scatter.4.cloned.1.call-start = ((), (), s32[]{:S(2)}) async-start(), calls=%async_computation.5 | async-start | bytes 737280
  166.8 1.3 copy-start
  177.5 38.5 %copy-start.2 = (bf16[1024,128]{1,0:T(8,128)(2,1)S(1)}, bf16[1024,128]{1,0:T(8,128)(2,1)}, u32[]{:S(2)}) copy-start(bf16[1024,128]{1,0:T(8,128)(2,1)} %w_ref.2) | copy-start | bytes 786436
  210.5 29.6 %all-to-all-start.3 = ((bf16[256,2,640]{2,1,0:T(2,128)(2,1)}), bf16[256,2,640]{2,1,0:T(2,128)(2,1)S(1)}, u32[]{:S(2)}, u32[]{:S(2)}) async-start(bf16[256,2,640]{2,1,0:T(2,128)(2,1)} %totals.1), calls=%async_computation.3 | async-start | bytes 1310720 | tf_op jit(solution)/shard_map/all_to_all | solution.py:516
Sparse Core Ops, SparseCore 0:
  125.0 33.7 reduce-scatter.3

commit v4 on v3

--- a/solution.py
+++ b/solution.py
@@ -542,6 +542,17 @@
     )(got)
 
 
+def scatter_dp(x, n_dp):
+    d = lax.axis_index("dp")
+    for bit in reversed(range(n_dp.bit_length() - 1)):
+        half = x.shape[0] // 2
+        b = (d >> bit) & 1
+        keep = lax.dynamic_slice_in_dim(x, b * half, half, 0)
+        give = lax.dynamic_slice_in_dim(x, (1 - b) * half, half, 0)
+        x = keep + lax.ppermute(give, "dp", [(k, k ^ (1 << bit)) for k in range(n_dp)])
+    return x
+
+
 def share_out(part, fold):
     share, cols = part.shape
     tall = jnp.pad(part.T.astype(BF), ((0, -cols % fold), (0, 0)))
@@ -578,7 +589,7 @@
         n = n_dp * n_graph
         fold = 2 * n
         small = weights_kernel(agg_t, g_pre, g_basis, trip, n)
-        part = lax.psum_scatter(small, "dp", scatter_dimension=0, tiled=True)
+        part = scatter_dp(small, n_dp)
         returned, piece = lax.optimization_barrier((returned, share_out(part, fold)))
         g_down_t, slab = return_kernel(returned, send_rows, edge_rows, piece)
         reduced = reduce_all(slab, n_dp, n_graph, feats, width // fold * feats)

time: 250 us -> 237 us (0.948)
  between operations: 14.1 us -> 0.76 us
  waiting for transfers between devices: 93.6 us -> 85.5 us
  starting transfers between devices: 25.1 us -> 32.2 us
    unnamed x2 -> x0, waiting for transfers between devices: 34 us -> none
    all_to_all x3, waiting for transfers between devices: 59.7 us -> 74.5 us  [exchange(): return lax.all_to_all(x, axes, split_axis=0, concat_axis=0, tiled=True)]
    ppermute x0 -> x3, waiting for transfers between devices: none -> 10.9 us  [scatter_dp(): lax.ppermute(give, 'dp', [(k, k ^ 1 << bit) for k in range(n_dp)])]
    ppermute x0 -> x3, starting transfers between devices: none -> 7.41 us  [scatter_dp(): lax.ppermute(give, 'dp', [(k, k ^ 1 << bit) for k in range(n_dp)])]
    unnamed x12 -> x11, local copies, waits for them, and re-layouts: 5.72 us -> 4.61 us
  transfers between devices with their start and end apart: 4 -> 6, of which waited for: 4 -> 6; matrix products, arithmetic and copies ran while one was open for 1% -> 2% of each run, Pallas kernels for 10% -> 10%
where the time goes in v4:
time: 237 us; the launch traced here: 236 us
  waiting for transfers between devices  85.5 us (36%)
  Pallas kernels  77.4 us (33%)
  starting transfers between devices  32.2 us (14%)
  blocking collectives  29.4 us (12%)
  local copies, waits for them, and re-layouts  8.61 us (4%)
  other arithmetic  2.52 us (1%)
    all_to_all x3, waiting for transfers between devices, exchange(): return lax.all_to_all(x, axes, split_axis=0, concat_axis=0, tiled=True)  74.5 us
    all_to_all x1, blocking collectives, exchange(): return lax.all_to_all(x, axes, split_axis=0, concat_axis=0, tiled=True)  29.4 us
    all_to_all x3, starting transfers between devices, exchange(): return lax.all_to_all(x, axes, split_axis=0, concat_axis=0, tiled=True)  24.8 us
    pallas_call x1, Pallas kernels, backward_kernel(): pl.pallas_call(body, out_shape=(jax.ShapeDtypeStruct((peers, feats, LO),...  14.2 us
    pallas_call x1, Pallas kernels, sort_kernel(): pl.pallas_call(body, out_shape=(jax.ShapeDtypeStruct((chunks, rows, LO),...  13.7 us
    pallas_call x1, Pallas kernels, forward_kernel(): pl.pallas_call(body, out_shape=(jax.ShapeDtypeStruct((chunks, feats, LO),...  11.3 us
    ppermute x3, waiting for transfers between devices, scatter_dp(): lax.ppermute(give, 'dp', [(k, k ^ 1 << bit) for k in range(n_dp)])  10.9 us
    pallas_call x1, Pallas kernels, return_kernel(): pl.pallas_call(body, out_shape=(jax.ShapeDtypeStruct((feats, n_edges), BF...  9.38 us
  transfers between devices with their start and end apart: 6, of which 6 were waited for; matrix products, arithmetic and copies ran while one was open for 2% of the time, Pallas kernels for 10%

profile of v4, /device:TPU:1, one launch (start us, length us, event | category | flops | bytes accessed | tf_op | source)
XLA Modules:
  0.0 236.3 jit_solution(15978064655091213581)
XLA Ops:
  0.6 9.0 %send.1 = bf16[32,128,256]{2,1,0:T(8,128)(2,1)} custom-call(bf16[2048,1024]{1,0:T(8,128)(2,1)} %bitcast.10, bf16[1024,128]{1,0:T(8,128)(2,1)} %w_ref.2, s32[1,8192]{1,0:T(1,128)} %i_ref.3), custom_call_target="tpu_custom_call" | custom-call | tf_op jit(solution)/shard_map/send/pallas_call | solution.py:76
  9.7 12.3 %all-to-all-start = ((bf16[32,128,256]{2,1,0:T(8,128)(2,1)}), bf16[32,128,256]{2,1,0:T(8,128)(2,1)S(1)}, u32[]{:S(2)}, u32[]{:S(2)}) async-start(bf16[32,128,256]{2,1,0:T(8,128)(2,1)} %send.1), calls=%async_computation | async-start | bytes 4194304 | tf_op jit(solution)/shard_map/all_to_all | solution.py:516
  22.8 13.7 %order.1 = (f32[32,48,256]{2,1,0:T(8,128)}, s32[2,128]{1,0:T(2,128)}) custom-call(s32[1,8192]{1,0:T(1,128)} %s_ref, s32[1,8192]{1,0:T(1,128)} %d_ref.1, bf16[42,8192]{1,0:T(8,128)(2,1)} %bitcast.15), custom_call_target="tpu_custom_call" | custom-call | tf_op jit(solution)/shard_map/order/pallas_call | solution.py:150
  36.5 34.2 %all-to-all-done.r_ref = bf16[32,128,256]{2,1,0:T(8,128)(2,1)S(1)} async-done(((bf16[32,128,256]{2,1,0:T(8,128)(2,1)}), bf16[32,128,256]{2,1,0:T(8,128)(2,1)S(1)}, u32[]{:S(2)}, u32[]{:S(2)}) %all-to-all-start) | async-done | bytes 2097184 | tf_op jit(solution)/shard_map/all_to_all | solution.py:516
  70.7 1.3 copy-done.1
  72.0 11.3 %forward.1 = (bf16[32,128,256]{2,1,0:T(8,128)(2,1)}, bf16[128,2048]{1,0:T(8,128)(2,1)}) custom-call(s32[2,128]{1,0:T(2,128)} %get-tuple-element.18.rg, bf16[32,128,256]{2,1,0:T(8,128)(2,1)} %copy-done.1, f32[32,48,256]{2,1,0:T(8,128)} %get-tuple-element.19.x_ref, bf16[128,48]{1,0:T(8,128)(2,1)} %pad.12.w_ref), custom_call_target="tpu_custom_call" | custom-call | tf_op jit(solution)/shard_map/forward/pallas_call | solution.py:234
  83.3 7.1 %dense.1 = (bf16[2048,1024]{1,0:T(8,128)(2,1)}, bf16[128,2048]{1,0:T(8,128)(2,1)}) custom-call(bf16[128,2048]{1,0:T(8,128)(2,1)} %get-tuple-element.20.a_ref, bf16[128,1024]{1,0:T(8,128)(2,1)} %w_ref.3, bf16[2048,1024]{1,0:T(8,128)(2,1)} %bitcast.12), custom_call_target="tpu_custom_call" | custom-call | tf_op jit(solution)/shard_map/dense/pallas_call | solution.py:279
  90.4 14.2 %backward.1 = (bf16[32,128,256]{2,1,0:T(8,128)(2,1)}, f32[32,128,256]{2,1,0:T(8,128)}) custom-call(s32[2,128]{1,0:T(2,128)} %get-tuple-element.18.rg, bf16[128,2048]{1,0:T(8,128)(2,1)} %get-tuple-element.21.g_ref, bf16[32,128,256]{2,1,0:T(8,128)(2,1)} %get-tuple-element.22.st_ref, f32[32,48,256]{2,1,0:T(8,128)} %get-tuple-element.19.x_ref, ...), custom_call_target="tpu_custom_call" | custom-call | tf_op jit(solution)/shard_map/backward/pallas_call | solution.py:349
  104.6 7.0 %all-to-all-start.1 = ((bf16[32,128,256]{2,1,0:T(8,128)(2,1)}), bf16[32,128,256]{2,1,0:T(8,128)(2,1)S(1)}, u32[]{:S(2)}, u32[]{:S(2)}) async-start(bf16[32,128,256]{2,1,0:T(8,128)(2,1)} %get-tuple-element.23), calls=%async_computation.1 | async-start | bytes 4194304 | tf_op jit(solution)/shard_map/all_to_all | solution.py:516
  111.6 6.5 %weights.1 = f32[128,1280]{1,0:T(8,128)} custom-call(bf16[128,2048]{1,0:T(8,128)(2,1)} %get-tuple-element.20.a_ref, bf16[2048,1024]{1,0:T(8,128)(2,1)} %get-tuple-element.24.p_ref, f32[32,128,256]{2,1,0:T(8,128)} %get-tuple-element.25.g_ref, f32[32,48,256]{2,1,0:T(8,128)} %get-tuple-element.19.x_ref), custom_call_target="tpu_custom_call" | custom-call | tf_op jit(solution)/shard_map/weights/pallas_call | solution.py:408
  119.1 3.0 %collective-permute-start = (f32[64,1280]{1,0:T(8,128)S(1)}, f32[64,1280]{1,0:T(8,128)S(1)}, u32[]{:S(2)}, u32[]{:S(2)}) collective-permute-start(f32[64,1280]{1,0:T(8,128)S(1)} %constant_dynamic-slice_fusion.2), channel_id=1, source_target_pairs={{0,128},{32,160},{64,192},{96,224},{128,0},{160,32},{192,64},{224,... | collective-permute-start | bytes 983048 | tf_op jit(solution)/shard_map/ppermute | solution.py:552
  122.2 6.7 %collective-permute-done = f32[64,1280]{1,0:T(8,128)S(1)} collective-permute-done((f32[64,1280]{1,0:T(8,128)S(1)}, f32[64,1280]{1,0:T(8,128)S(1)}, u32[]{:S(2)}, u32[]{:S(2)}) %collective-permute-start) | collective-permute-done | bytes 327712 | tf_op jit(solution)/shard_map/ppermute | solution.py:552
  129.9 1.3 collective-permute-start.1
  131.2 3.3 %collective-permute-done.1 = f32[32,1280]{1,0:T(8,128)S(1)} collective-permute-done((f32[32,1280]{1,0:T(8,128)S(1)}, f32[32,1280]{1,0:T(8,128)S(1)}, u32[]{:S(2)}, u32[]{:S(2)}) %collective-permute-start.1) | collective-permute-done | bytes 163872 | tf_op jit(solution)/shard_map/ppermute | solution.py:552
  134.5 3.1 %collective-permute-start.2 = (f32[16,1280]{1,0:T(8,128)S(1)}, f32[16,1280]{1,0:T(8,128)S(1)}, u32[]{:S(2)}, u32[]{:S(2)}) collective-permute-start(f32[16,1280]{1,0:T(8,128)S(1)} %constant_dynamic-slice_fusion), channel_id=1, source_target_pairs={{0,32},{32,0},{64,96},{96,64},{128,160},{160,128},{192,224},{224,1... | collective-permute-start | bytes 245768 | tf_op jit(solution)/shard_map/ppermute | solution.py:552
  139.4 20.9 %all-to-all-done.1.r_ref = bf16[32,128,256]{2,1,0:T(8,128)(2,1)S(1)} async-done(((bf16[32,128,256]{2,1,0:T(8,128)(2,1)}), bf16[32,128,256]{2,1,0:T(8,128)(2,1)S(1)}, u32[]{:S(2)}, u32[]{:S(2)}) %all-to-all-start.1) | async-done | bytes 2097184 | tf_op jit(solution)/shard_map/all_to_all | solution.py:516
  160.3 1.3 copy-done
  161.6 9.4 %returned.1 = (bf16[128,2048]{1,0:T(8,128)(2,1)}, bf16[512,384]{1,0:T(8,128)(2,1)}) custom-call(bf16[32,128,256]{2,1,0:T(8,128)(2,1)} %copy-done, s32[1,8192]{1,0:T(1,128)} %i_ref.3, bf16[2048,1024]{1,0:T(8,128)(2,1)} %bitcast.11, bf16[512,128]{1,0:T(8,128)(2,1)} %pad.14.p_ref), custom_call_target="tpu_custom_call" | custom-call | tf_op jit(solution)/shard_map/returned/pallas_call | solution.py:471
  171.0 1.2 reshape.14
  172.2 29.4 %all_to_all.20.x_ref = bf16[256,2,384]{2,1,0:T(2,128)(2,1)} all-to-all(bf16[256,2,384]{2,1,0:T(2,128)(2,1)S(1)} %reshape.14), channel_id=1, replica_groups=mesh['dp'=8,'graph'=32] {'dp','graph'}, dimensions={0} | all-to-all | bytes 786432 | tf_op jit(solution)/shard_map/all_to_all | solution.py:516
  201.6 2.4 %totals.1 = bf16[256,2,640]{2,1,0:T(2,128)(2,1)} custom-call(bf16[256,2,384]{2,1,0:T(2,128)(2,1)} %all_to_all.20.x_ref), custom_call_target="tpu_custom_call" | custom-call | tf_op jit(solution)/shard_map/totals/pallas_call | solution.py:537
  203.9 5.5 %all-to-all-start.3 = ((bf16[256,2,640]{2,1,0:T(2,128)(2,1)}), bf16[256,2,640]{2,1,0:T(2,128)(2,1)S(1)}, u32[]{:S(2)}, u32[]{:S(2)}) async-start(bf16[256,2,640]{2,1,0:T(2,128)(2,1)} %totals.1), calls=%async_computation.3 | async-start | bytes 1310720 | tf_op jit(solution)/shard_map/all_to_all | solution.py:516
  210.3 3.8 %grad_edges.1 = bf16[2048,1024]{1,0:T(8,128)(2,1)} custom-call(bf16[128,2048]{1,0:T(8,128)(2,1)} %get-tuple-element.28.g_ref, bf16[128,1024]{1,0:T(8,128)(2,1)} %bitcast.14), custom_call_target="tpu_custom_call" | custom-call | tf_op jit(solution)/shard_map/grad_edges/pallas_call | solution.py:504
  214.1 19.4 %all-to-all-done.3 = bf16[256,2,640]{2,1,0:T(2,128)(2,1)S(1)} async-done(((bf16[256,2,640]{2,1,0:T(2,128)(2,1)}), bf16[256,2,640]{2,1,0:T(2,128)(2,1)S(1)}, u32[]{:S(2)}, u32[]{:S(2)}) %all-to-all-start.3) | async-done | bytes 655392 | tf_op jit(solution)/shard_map/all_to_all | solution.py:516
  (25 shorter events, 8.2 us)
Async XLA Ops:
  9.7 12.3 %copy-start.3 = (bf16[42,128]{1,0:T(8,128)(2,1)S(1)}, bf16[42,128]{1,0:T(8,128)(2,1)}, u32[]{:S(2)}) copy-start(bf16[42,128]{1,0:T(8,128)(2,1)} %param.17) | copy-start | bytes 32260
  9.7 61.0 %all-to-all-start = ((bf16[32,128,256]{2,1,0:T(8,128)(2,1)}), bf16[32,128,256]{2,1,0:T(8,128)(2,1)S(1)}, u32[]{:S(2)}, u32[]{:S(2)}) async-start(bf16[32,128,256]{2,1,0:T(8,128)(2,1)} %send.1), calls=%async_computation | async-start | bytes 4194304 | tf_op jit(solution)/shard_map/all_to_all | solution.py:516
  70.7 1.3 copy-start.1
  104.6 55.7 %all-to-all-start.1 = ((bf16[32,128,256]{2,1,0:T(8,128)(2,1)}), bf16[32,128,256]{2,1,0:T(8,128)(2,1)S(1)}, u32[]{:S(2)}, u32[]{:S(2)}) async-start(bf16[32,128,256]{2,1,0:T(8,128)(2,1)} %get-tuple-element.23), calls=%async_computation.1 | async-start | bytes 4194304 | tf_op jit(solution)/shard_map/all_to_all | solution.py:516
  119.1 9.8 %collective-permute-start = (f32[64,1280]{1,0:T(8,128)S(1)}, f32[64,1280]{1,0:T(8,128)S(1)}, u32[]{:S(2)}, u32[]{:S(2)}) collective-permute-start(f32[64,1280]{1,0:T(8,128)S(1)} %constant_dynamic-slice_fusion.2), channel_id=1, source_target_pairs={{0,128},{32,160},{64,192},{96,224},{128,0},{160,32},{192,64},{224,... | collective-permute-start | bytes 983048 | tf_op jit(solution)/shard_map/ppermute | solution.py:552
  129.9 4.6 %collective-permute-start.1 = (f32[32,1280]{1,0:T(8,128)S(1)}, f32[32,1280]{1,0:T(8,128)S(1)}, u32[]{:S(2)}, u32[]{:S(2)}) collective-permute-start(f32[32,1280]{1,0:T(8,128)S(1)} %constant_dynamic-slice_fusion.1), channel_id=1, source_target_pairs={{0,64},{32,96},{64,0},{96,32},{128,192},{160,224},{192,128},{224,1... | collective-permute-start | bytes 491528 | tf_op jit(solution)/shard_map/ppermute | solution.py:552
  134.5 4.0 %collective-permute-start.2 = (f32[16,1280]{1,0:T(8,128)S(1)}, f32[16,1280]{1,0:T(8,128)S(1)}, u32[]{:S(2)}, u32[]{:S(2)}) collective-permute-start(f32[16,1280]{1,0:T(8,128)S(1)} %constant_dynamic-slice_fusion), channel_id=1, source_target_pairs={{0,32},{32,0},{64,96},{96,64},{128,160},{160,128},{192,224},{224,1... | collective-permute-start | bytes 245768 | tf_op jit(solution)/shard_map/ppermute | solution.py:552
  160.3 1.3 copy-start
  171.0 38.4 %copy-start.2 = (bf16[1024,128]{1,0:T(8,128)(2,1)S(1)}, bf16[1024,128]{1,0:T(8,128)(2,1)}, u32[]{:S(2)}) copy-start(bf16[1024,128]{1,0:T(8,128)(2,1)} %w_ref.2) | copy-start | bytes 786436
  203.9 29.6 %all-to-all-start.3 = ((bf16[256,2,640]{2,1,0:T(2,128)(2,1)}), bf16[256,2,640]{2,1,0:T(2,128)(2,1)S(1)}, u32[]{:S(2)}, u32[]{:S(2)}) async-start(bf16[256,2,640]{2,1,0:T(2,128)(2,1)} %totals.1), calls=%async_computation.3 | async-start | bytes 1310720 | tf_op jit(solution)/shard_map/all_to_all | solution.py:516

commit v5 on v4

--- a/solution.py
+++ b/solution.py
@@ -198,11 +198,9 @@
             far = jnp.maximum(far, rg[1, i * per + a] - b0)
             hot = onehot(ids(a, 0), LO)
             hi = ids(a, 1)
-            got = jnp.zeros((feats, LO), F32)
-            for n in range(NEAR):
-                res = nn(r_ref[jnp.minimum(b0 + n, peers - 1)], hot)
-                got = jnp.where(hi == b0 + n, res, got)
-            source[a] = got
+            at = jnp.minimum(b0, peers - NEAR)
+            near = r_ref[pl.ds(at, NEAR)].reshape(NEAR * feats, LO)
+            source[a] = pick(nn(near, hot), hi, NEAR, feats, at)
 
         @pl.when(far >= NEAR)
         def _():
@@ -241,7 +239,7 @@
             num_scalar_prefetch=1,
             grid=(steps,),
             in_specs=[
-                whole(recv.shape),
+                pl.BlockSpec(memory_space=pltpu.VMEM),
                 pl.BlockSpec((per, rows, LO), lambda i, rg: (i, 0, 0)),
                 whole(w_basis_t.shape),
             ],
@@ -326,9 +324,9 @@
             far = jnp.maximum(far, rg[1, i * per + a] - b0)
             hot = onehot(ids(a, 0), LO)
             hi = ids(a, 1)
-            for n in range(NEAR):
-                res = nt(jnp.where(hi == b0 + n, source[a], 0.0).astype(BF), hot)
-                acc[jnp.minimum(b0 + n, peers - 1)] += res
+            at = jnp.minimum(b0, peers - NEAR)
+            near = jnp.concatenate([jnp.where(hi == at + n, source[a], 0.0) for n in range(NEAR)]).astype(BF)
+            acc[pl.ds(at, NEAR)] += nt(near, hot).reshape(NEAR, feats, LO)
 
         @pl.when(far >= NEAR)
         def _():
@@ -446,7 +444,7 @@
             for a in range(per):
                 cols = slice(a * slot, (a + 1) * slot)
                 lo, hi = split(i_ref[:, cols])
-                rows = r_ref[a].astype(F32)
+                rows = r_ref[i * per + a].astype(F32)
                 for j in range(eblocks):
                     pm[j * feats:(j + 1) * feats, cols] = jnp.where(hi == j, rows, 0.0).astype(BF)
                 oh[:, cols] = onehot(lo, slot)
@@ -476,7 +474,7 @@
         ),
         grid=(steps + esteps,),
         in_specs=[
-            pl.BlockSpec((per, feats, slot), lambda i: (jnp.minimum(i, steps - 1), 0, 0)),
+            pl.BlockSpec(memory_space=pltpu.VMEM),
             pl.BlockSpec((1, per * slot), lambda i: (0, jnp.minimum(i, steps - 1))),
             pl.BlockSpec((eb, width), lambda i: (jnp.maximum(i - steps, 0), 0)),
             full(piece.shape),
@@ -576,7 +574,7 @@
         feats = w_down.shape[1]
         nb = basis.shape[0]
         sent = send_kernel(edge_rows, w_down, send_rows, n_graph)
-        received = exchange(sent, "graph")
+        received = pltpu.with_memory_space_constraint(exchange(sent, "graph"), pltpu.VMEM)
         src, sent_now = lax.optimization_barrier((trip_src, sent))
         trip, ranges = sort_kernel(src, trip_dst, basis, n_graph)
         w_basis_t = jnp.pad(w_basis.T, ((0, 0), (0, trip.shape[1] - nb)))
@@ -591,6 +589,7 @@
         small = weights_kernel(agg_t, g_pre, g_basis, trip, n)
         part = scatter_dp(small, n_dp)
         returned, piece = lax.optimization_barrier((returned, share_out(part, fold)))
+        returned = pltpu.with_memory_space_constraint(returned, pltpu.VMEM)
         g_down_t, slab = return_kernel(returned, send_rows, edge_rows, piece)
         reduced = reduce_all(slab, n_dp, n_graph, feats, width // fold * feats)
         grad_edges = edges_kernel(g_down_t, w_down.T)

time: 237 us -> 231 us (0.975)
  Pallas kernels: 77.4 us -> 74.1 us
  local copies, waits for them, and re-layouts: 8.61 us -> 5.97 us
    unnamed x11 -> x7, local copies, waits for them, and re-layouts: 4.61 us -> 1.98 us
where the time goes in v5:
time: 231 us; the launch traced here: 230 us
  waiting for transfers between devices  85.4 us (37%)
  Pallas kernels  74.1 us (32%)
  starting transfers between devices  32.3 us (14%)
  blocking collectives  29.4 us (13%)
  local copies, waits for them, and re-layouts  5.97 us (3%)
  other arithmetic  2.52 us (1%)
    all_to_all x3, waiting for transfers between devices, exchange(): return lax.all_to_all(x, axes, split_axis=0, concat_axis=0, tiled=True)  74.6 us
    all_to_all x1, blocking collectives, exchange(): return lax.all_to_all(x, axes, split_axis=0, concat_axis=0, tiled=True)  29.4 us
    all_to_all x3, starting transfers between devices, exchange(): return lax.all_to_all(x, axes, split_axis=0, concat_axis=0, tiled=True)  24.8 us
    pallas_call x1, Pallas kernels, sort_kernel(): pl.pallas_call(body, out_shape=(jax.ShapeDtypeStruct((chunks, rows, LO),...  13.7 us
    pallas_call x1, Pallas kernels, backward_kernel(): pl.pallas_call(body, out_shape=(jax.ShapeDtypeStruct((peers, feats, LO),...  12.3 us
    ppermute x3, waiting for transfers between devices, scatter_dp(): lax.ppermute(give, 'dp', [(k, k ^ 1 << bit) for k in range(n_dp)])  10.9 us
    pallas_call x1, Pallas kernels, forward_kernel(): pl.pallas_call(body, out_shape=(jax.ShapeDtypeStruct((chunks, feats, LO),...  10.5 us
    pallas_call x1, Pallas kernels, send_kernel(): pl.pallas_call(body, out_shape=jax.ShapeDtypeStruct((peers, feats, slot),...  9.03 us
  transfers between devices with their start and end apart: 6, of which 6 were waited for; matrix products, arithmetic and copies ran while one was open for 2% of the time, Pallas kernels for 10%

profile of v5, /device:TPU:1, one launch (start us, length us, event | category | flops | bytes accessed | tf_op | source)
XLA Modules:
  0.0 230.5 jit_solution(7698866960089499136)
XLA Ops:
  0.6 9.0 %send.1 = bf16[32,128,256]{2,1,0:T(8,128)(2,1)} custom-call(bf16[2048,1024]{1,0:T(8,128)(2,1)} %bitcast.10, bf16[1024,128]{1,0:T(8,128)(2,1)} %w_ref.2, s32[1,8192]{1,0:T(1,128)} %i_ref.3), custom_call_target="tpu_custom_call" | custom-call | tf_op jit(solution)/shard_map/send/pallas_call | solution.py:76
  9.7 12.3 %all-to-all-start = ((bf16[32,128,256]{2,1,0:T(8,128)(2,1)}), bf16[32,128,256]{2,1,0:T(8,128)(2,1)S(1)}, u32[]{:S(2)}, u32[]{:S(2)}) async-start(bf16[32,128,256]{2,1,0:T(8,128)(2,1)} %send.1), calls=%async_computation | async-start | bytes 4194304 | tf_op jit(solution)/shard_map/all_to_all | solution.py:514
  22.8 13.7 %order.1 = (f32[32,48,256]{2,1,0:T(8,128)}, s32[2,128]{1,0:T(2,128)}) custom-call(s32[1,8192]{1,0:T(1,128)} %s_ref, s32[1,8192]{1,0:T(1,128)} %d_ref.1, bf16[42,8192]{1,0:T(8,128)(2,1)} %bitcast.15), custom_call_target="tpu_custom_call" | custom-call | tf_op jit(solution)/shard_map/order/pallas_call | solution.py:150
  36.5 34.2 %all-to-all-done.r_ref = bf16[32,128,256]{2,1,0:T(8,128)(2,1)S(1)} async-done(((bf16[32,128,256]{2,1,0:T(8,128)(2,1)}), bf16[32,128,256]{2,1,0:T(8,128)(2,1)S(1)}, u32[]{:S(2)}, u32[]{:S(2)}) %all-to-all-start) | async-done | bytes 2097184 | tf_op jit(solution)/shard_map/all_to_all | solution.py:514
  70.7 10.5 %forward.1 = (bf16[32,128,256]{2,1,0:T(8,128)(2,1)}, bf16[128,2048]{1,0:T(8,128)(2,1)}) custom-call(s32[2,128]{1,0:T(2,128)} %get-tuple-element.18.rg, bf16[32,128,256]{2,1,0:T(8,128)(2,1)S(1)} %all-to-all-done.r_ref, f32[32,48,256]{2,1,0:T(8,128)} %get-tuple-element.19.x_ref, bf16[128,48]{1,0:T(8,128)(2,1)} %pad.12.w_ref), custom_call_target="tpu_custom_call" | custom-call | tf_op jit(solution)/shard_map/forward/pallas_call | solution.py:232
  81.2 7.1 %dense.1 = (bf16[2048,1024]{1,0:T(8,128)(2,1)}, bf16[128,2048]{1,0:T(8,128)(2,1)}) custom-call(bf16[128,2048]{1,0:T(8,128)(2,1)} %get-tuple-element.20.a_ref, bf16[128,1024]{1,0:T(8,128)(2,1)} %w_ref.3, bf16[2048,1024]{1,0:T(8,128)(2,1)} %bitcast.12), custom_call_target="tpu_custom_call" | custom-call | tf_op jit(solution)/shard_map/dense/pallas_call | solution.py:277
  88.3 12.3 %backward.1 = (bf16[32,128,256]{2,1,0:T(8,128)(2,1)}, f32[32,128,256]{2,1,0:T(8,128)}) custom-call(s32[2,128]{1,0:T(2,128)} %get-tuple-element.18.rg, bf16[128,2048]{1,0:T(8,128)(2,1)} %get-tuple-element.21.g_ref, bf16[32,128,256]{2,1,0:T(8,128)(2,1)} %get-tuple-element.22.st_ref, f32[32,48,256]{2,1,0:T(8,128)} %get-tuple-element.19.x_ref, ...), custom_call_target="tpu_custom_call" | custom-call | tf_op jit(solution)/shard_map/backward/pallas_call | solution.py:347
  100.7 7.0 %all-to-all-start.1 = ((bf16[32,128,256]{2,1,0:T(8,128)(2,1)}), bf16[32,128,256]{2,1,0:T(8,128)(2,1)S(1)}, u32[]{:S(2)}, u32[]{:S(2)}) async-start(bf16[32,128,256]{2,1,0:T(8,128)(2,1)} %get-tuple-element.23), calls=%async_computation.1 | async-start | bytes 4194304 | tf_op jit(solution)/shard_map/all_to_all | solution.py:514
  107.7 6.5 %weights.1 = f32[128,1280]{1,0:T(8,128)} custom-call(bf16[128,2048]{1,0:T(8,128)(2,1)} %get-tuple-element.20.a_ref, bf16[2048,1024]{1,0:T(8,128)(2,1)} %get-tuple-element.24.p_ref, f32[32,128,256]{2,1,0:T(8,128)} %get-tuple-element.25.g_ref, f32[32,48,256]{2,1,0:T(8,128)} %get-tuple-element.19.x_ref), custom_call_target="tpu_custom_call" | custom-call | tf_op jit(solution)/shard_map/weights/pallas_call | solution.py:406
  115.2 2.9 %collective-permute-start = (f32[64,1280]{1,0:T(8,128)S(1)}, f32[64,1280]{1,0:T(8,128)S(1)}, u32[]{:S(2)}, u32[]{:S(2)}) collective-permute-start(f32[64,1280]{1,0:T(8,128)S(1)} %constant_dynamic-slice_fusion.2), channel_id=1, source_target_pairs={{0,128},{32,160},{64,192},{96,224},{128,0},{160,32},{192,64},{224,... | collective-permute-start | bytes 983048 | tf_op jit(solution)/shard_map/ppermute | solution.py:550
  118.0 6.7 %collective-permute-done = f32[64,1280]{1,0:T(8,128)S(1)} collective-permute-done((f32[64,1280]{1,0:T(8,128)S(1)}, f32[64,1280]{1,0:T(8,128)S(1)}, u32[]{:S(2)}, u32[]{:S(2)}) %collective-permute-start) | collective-permute-done | bytes 327712 | tf_op jit(solution)/shard_map/ppermute | solution.py:550
  124.7 1.0 dynamic-slice_add_fusion
  125.7 1.5 collective-permute-start.1
  127.3 3.2 %collective-permute-done.1 = f32[32,1280]{1,0:T(8,128)S(1)} collective-permute-done((f32[32,1280]{1,0:T(8,128)S(1)}, f32[32,1280]{1,0:T(8,128)S(1)}, u32[]{:S(2)}, u32[]{:S(2)}) %collective-permute-start.1) | collective-permute-done | bytes 163872 | tf_op jit(solution)/shard_map/ppermute | solution.py:550
  130.6 3.1 %collective-permute-start.2 = (f32[16,1280]{1,0:T(8,128)S(1)}, f32[16,1280]{1,0:T(8,128)S(1)}, u32[]{:S(2)}, u32[]{:S(2)}) collective-permute-start(f32[16,1280]{1,0:T(8,128)S(1)} %constant_dynamic-slice_fusion), channel_id=1, source_target_pairs={{0,32},{32,0},{64,96},{96,64},{128,160},{160,128},{192,224},{224,1... | collective-permute-start | bytes 245768 | tf_op jit(solution)/shard_map/ppermute | solution.py:550
  135.4 20.9 %all-to-all-done.1.r_ref = bf16[32,128,256]{2,1,0:T(8,128)(2,1)S(1)} async-done(((bf16[32,128,256]{2,1,0:T(8,128)(2,1)}), bf16[32,128,256]{2,1,0:T(8,128)(2,1)S(1)}, u32[]{:S(2)}, u32[]{:S(2)}) %all-to-all-start.1) | async-done | bytes 2097184 | tf_op jit(solution)/shard_map/all_to_all | solution.py:514
  156.4 8.7 %returned.1 = (bf16[128,2048]{1,0:T(8,128)(2,1)}, bf16[512,384]{1,0:T(8,128)(2,1)}) custom-call(bf16[32,128,256]{2,1,0:T(8,128)(2,1)S(1)} %all-to-all-done.1.r_ref, s32[1,8192]{1,0:T(1,128)} %i_ref.3, bf16[2048,1024]{1,0:T(8,128)(2,1)} %bitcast.11, bf16[512,128]{1,0:T(8,128)(2,1)} %pad.14.p_ref), custom_call_target="tpu_custom_call" | custom-call | tf_op jit(solution)/shard_map/returned/pallas_call | solution.py:469
  165.1 1.2 reshape.14
  166.3 29.4 %all_to_all.20.x_ref = bf16[256,2,384]{2,1,0:T(2,128)(2,1)} all-to-all(bf16[256,2,384]{2,1,0:T(2,128)(2,1)S(1)} %reshape.14), channel_id=1, replica_groups=mesh['dp'=8,'graph'=32] {'dp','graph'}, dimensions={0} | all-to-all | bytes 786432 | tf_op jit(solution)/shard_map/all_to_all | solution.py:514
  195.7 2.4 %totals.1 = bf16[256,2,640]{2,1,0:T(2,128)(2,1)} custom-call(bf16[256,2,384]{2,1,0:T(2,128)(2,1)} %all_to_all.20.x_ref), custom_call_target="tpu_custom_call" | custom-call | tf_op jit(solution)/shard_map/totals/pallas_call | solution.py:535
  198.0 5.5 %all-to-all-start.3 = ((bf16[256,2,640]{2,1,0:T(2,128)(2,1)}), bf16[256,2,640]{2,1,0:T(2,128)(2,1)S(1)}, u32[]{:S(2)}, u32[]{:S(2)}) async-start(bf16[256,2,640]{2,1,0:T(2,128)(2,1)} %totals.1), calls=%async_computation.3 | async-start | bytes 1310720 | tf_op jit(solution)/shard_map/all_to_all | solution.py:514
  204.4 3.8 %grad_edges.1 = bf16[2048,1024]{1,0:T(8,128)(2,1)} custom-call(bf16[128,2048]{1,0:T(8,128)(2,1)} %get-tuple-element.28.g_ref, bf16[128,1024]{1,0:T(8,128)(2,1)} %bitcast.14), custom_call_target="tpu_custom_call" | custom-call | tf_op jit(solution)/shard_map/grad_edges/pallas_call | solution.py:502
  208.2 19.4 %all-to-all-done.3 = bf16[256,2,640]{2,1,0:T(2,128)(2,1)S(1)} async-done(((bf16[256,2,640]{2,1,0:T(2,128)(2,1)}), bf16[256,2,640]{2,1,0:T(2,128)(2,1)S(1)}, u32[]{:S(2)}, u32[]{:S(2)}) %all-to-all-start.3) | async-done | bytes 655392 | tf_op jit(solution)/shard_map/all_to_all | solution.py:514
  229.5 1.0 copy.21
  (21 shorter events, 6.2 us)
Async XLA Ops:
  9.7 12.3 %copy-start.1 = (bf16[42,128]{1,0:T(8,128)(2,1)S(1)}, bf16[42,128]{1,0:T(8,128)(2,1)}, u32[]{:S(2)}) copy-start(bf16[42,128]{1,0:T(8,128)(2,1)} %param.17) | copy-start | bytes 32260
  9.7 61.0 %all-to-all-start = ((bf16[32,128,256]{2,1,0:T(8,128)(2,1)}), bf16[32,128,256]{2,1,0:T(8,128)(2,1)S(1)}, u32[]{:S(2)}, u32[]{:S(2)}) async-start(bf16[32,128,256]{2,1,0:T(8,128)(2,1)} %send.1), calls=%async_computation | async-start | bytes 4194304 | tf_op jit(solution)/shard_map/all_to_all | solution.py:514
  100.7 55.7 %all-to-all-start.1 = ((bf16[32,128,256]{2,1,0:T(8,128)(2,1)}), bf16[32,128,256]{2,1,0:T(8,128)(2,1)S(1)}, u32[]{:S(2)}, u32[]{:S(2)}) async-start(bf16[32,128,256]{2,1,0:T(8,128)(2,1)} %get-tuple-element.23), calls=%async_computation.1 | async-start | bytes 4194304 | tf_op jit(solution)/shard_map/all_to_all | solution.py:514
  115.2 9.6 %collective-permute-start = (f32[64,1280]{1,0:T(8,128)S(1)}, f32[64,1280]{1,0:T(8,128)S(1)}, u32[]{:S(2)}, u32[]{:S(2)}) collective-permute-start(f32[64,1280]{1,0:T(8,128)S(1)} %constant_dynamic-slice_fusion.2), channel_id=1, source_target_pairs={{0,128},{32,160},{64,192},{96,224},{128,0},{160,32},{192,64},{224,... | collective-permute-start | bytes 983048 | tf_op jit(solution)/shard_map/ppermute | solution.py:550
  125.7 4.8 %collective-permute-start.1 = (f32[32,1280]{1,0:T(8,128)S(1)}, f32[32,1280]{1,0:T(8,128)S(1)}, u32[]{:S(2)}, u32[]{:S(2)}) collective-permute-start(f32[32,1280]{1,0:T(8,128)S(1)} %constant_dynamic-slice_fusion.1), channel_id=1, source_target_pairs={{0,64},{32,96},{64,0},{96,32},{128,192},{160,224},{192,128},{224,1... | collective-permute-start | bytes 491528 | tf_op jit(solution)/shard_map/ppermute | solution.py:550
  130.6 4.0 %collective-permute-start.2 = (f32[16,1280]{1,0:T(8,128)S(1)}, f32[16,1280]{1,0:T(8,128)S(1)}, u32[]{:S(2)}, u32[]{:S(2)}) collective-permute-start(f32[16,1280]{1,0:T(8,128)S(1)} %constant_dynamic-slice_fusion), channel_id=1, source_target_pairs={{0,32},{32,0},{64,96},{96,64},{128,160},{160,128},{192,224},{224,1... | collective-permute-start | bytes 245768 | tf_op jit(solution)/shard_map/ppermute | solution.py:550
  165.1 38.4 %copy-start = (bf16[1024,128]{1,0:T(8,128)(2,1)S(1)}, bf16[1024,128]{1,0:T(8,128)(2,1)}, u32[]{:S(2)}) copy-start(bf16[1024,128]{1,0:T(8,128)(2,1)} %w_ref.2) | copy-start | bytes 786436
  198.0 29.6 %all-to-all-start.3 = ((bf16[256,2,640]{2,1,0:T(2,128)(2,1)}), bf16[256,2,640]{2,1,0:T(2,128)(2,1)S(1)}, u32[]{:S(2)}, u32[]{:S(2)}) async-start(bf16[256,2,640]{2,1,0:T(2,128)(2,1)} %totals.1), calls=%async_computation.3 | async-start | bytes 1310720 | tf_op jit(solution)/shard_map/all_to_all | solution.py:514

commit v6 on v5

--- a/solution.py
+++ b/solution.py
@@ -423,8 +423,8 @@
 def return_kernel(ret, send_idx, edges, piece):
     peers, feats, slot = ret.shape
     n_edges, width = edges.shape
-    fold = piece.shape[0]
-    lanes = width // fold * feats + piece.shape[1]
+    own = width // peers
+    lines = own + piece.shape[1]
     per = 32
     steps = peers // per
     eblocks = n_edges // LO
@@ -462,15 +462,17 @@
 
         @pl.when(i == steps + esteps - 1)
         def _():
-            for q in range(width // fold):
-                grad_out[:, q * feats:(q + 1) * feats] = gacc[:, q * fold:(q + 1) * fold].T.astype(BF)
-            grad_out[:, width // fold * feats:] = p_ref[...]
+            for q in range(width // feats):
+                rows = gacc[:, q * feats:(q + 1) * feats].T.astype(BF)
+                for k in range(feats // own):
+                    grad_out[q * (feats // own) + k, :own] = rows[k * own:(k + 1) * own]
+            grad_out[:, own:] = p_ref[...]
 
     return pl.pallas_call(
         body,
         out_shape=(
             jax.ShapeDtypeStruct((feats, n_edges), BF),
-            jax.ShapeDtypeStruct((fold, lanes), BF),
+            jax.ShapeDtypeStruct((peers, lines, feats), BF),
         ),
         grid=(steps + esteps,),
         in_specs=[
@@ -479,7 +481,7 @@
             pl.BlockSpec((eb, width), lambda i: (jnp.maximum(i - steps, 0), 0)),
             full(piece.shape),
         ],
-        out_specs=(full((feats, n_edges)), full((fold, lanes))),
+        out_specs=(full((feats, n_edges)), full((peers, lines, feats))),
         scratch_shapes=[
             pltpu.VMEM((eblocks * feats, LO), F32),
             pltpu.VMEM((eblocks * feats, per * slot), BF),
@@ -514,29 +516,34 @@
     return lax.all_to_all(x, axes, split_axis=0, concat_axis=0, tiled=True)
 
 
-def total_kernel(got, n_dp, feats, own):
-    n, pair, lanes = got.shape
-    share = feats // n_dp
-    groups = (lanes - own) // feats * 3
-    out_lanes = own + groups * feats
-
+def graph_sum_kernel(got, n_dp):
     def body(x_ref, out_ref):
-        sums = jnp.sum(x_ref[...].astype(F32).reshape(n_dp, n // n_dp, pair, lanes), axis=1)
-        parts = [jnp.sum(sums[:, :, :own], axis=0)]
-        where = lax.broadcasted_iota(jnp.int32, (n_dp, pair, feats), 2) // share
-        mine = where == lax.broadcasted_iota(jnp.int32, (n_dp, pair, feats), 0)
-        for q in range(groups):
-            piece = sums[:, :, own + q * share:own + (q + 1) * share]
-            wide = jnp.concatenate([piece] * n_dp, axis=2)
-            parts.append(jnp.sum(jnp.where(mine, wide, 0.0), axis=0))
-        row = jnp.concatenate(parts, axis=1).astype(BF)
-        out_ref[...] = jnp.broadcast_to(row[None], out_ref.shape)
-
-    return pl.pallas_call(
-        body,
-        out_shape=jax.ShapeDtypeStruct((n, pair, out_lanes), BF),
-        compiler_params=params(),
-        name="totals",
+        mine = jnp.sum(x_ref[...].astype(F32), axis=0).astype(BF)
+        out_ref[...] = jnp.broadcast_to(mine[None], out_ref.shape)
+
+    return pl.pallas_call(
+        body,
+        out_shape=jax.ShapeDtypeStruct((n_dp,) + got.shape[1:], BF),
+        compiler_params=params(),
+        name="graph_sum",
+    )(got)
+
+
+def dp_sum_kernel(got, n_graph, own, cols):
+    n_dp, lines, feats = got.shape
+
+    def body(x_ref, out_ref):
+        x = x_ref[...].astype(F32)
+        down = jnp.sum(x[:, :own], axis=0)
+        rest = x[:, own:].reshape(n_dp * (lines - own), feats).T
+        mine = jnp.concatenate([down, rest[:cols]]).astype(BF)
+        out_ref[...] = jnp.broadcast_to(mine[None], out_ref.shape)
+
+    return pl.pallas_call(
+        body,
+        out_shape=jax.ShapeDtypeStruct((n_graph, own + cols, feats), BF),
+        compiler_params=params(),
+        name="dp_sum",
     )(got)
 
 
@@ -551,19 +558,13 @@
     return x
 
 
-def share_out(part, fold):
+def share_out(part, width, peers):
     share, cols = part.shape
-    tall = jnp.pad(part.T.astype(BF), ((0, -cols % fold), (0, 0)))
-    wide = jnp.concatenate([tall[k:k + fold] for k in range(0, tall.shape[0], fold)], axis=1)
-    return jnp.pad(wide, ((0, 0), (0, -wide.shape[1] % 128)))
-
-
-def reduce_all(slab, n_dp, n_graph, feats, own):
-    n = n_dp * n_graph
-    axes = ("dp", "graph")
-    got = exchange(slab.reshape(n, slab.shape[0] // n, slab.shape[1]), axes)
-    sent = total_kernel(got, n_dp, feats, own)
-    return exchange(sent, axes).reshape(slab.shape[0], sent.shape[2])
+    part = part.astype(BF)
+    views = [part[:, :width], part[:, width:]]
+    views = [v.reshape(share, peers, -1).transpose(1, 0, 2) for v in views]
+    wide = jnp.concatenate(views, axis=2)
+    return jnp.pad(wide, ((0, 0), (0, 0), (0, -wide.shape[2] % 128)))
 
 
 def make_shards(n_dp, n_graph):
@@ -585,19 +586,19 @@
         )
         returned = exchange(g_received, "graph")
         n = n_dp * n_graph
-        fold = 2 * n
         small = weights_kernel(agg_t, g_pre, g_basis, trip, n)
         part = scatter_dp(small, n_dp)
-        returned, piece = lax.optimization_barrier((returned, share_out(part, fold)))
+        returned, piece = lax.optimization_barrier((returned, share_out(part, width, n_graph)))
         returned = pltpu.with_memory_space_constraint(returned, pltpu.VMEM)
         g_down_t, slab = return_kernel(returned, send_rows, edge_rows, piece)
-        reduced = reduce_all(slab, n_dp, n_graph, feats, width // fold * feats)
+        own = width // n_graph
+        cols = small.shape[1] // n_graph
+        shared = exchange(graph_sum_kernel(exchange(slab, "graph"), n_dp), "dp")
+        reduced = exchange(dp_sum_kernel(shared, n_graph, own, cols), "graph")
         grad_edges = edges_kernel(g_down_t, w_down.T)
-        parts = [reduced[:, k * feats:(k + 1) * feats] for k in range(reduced.shape[1] // feats)]
-        per = width // fold
-        grad_down = jnp.concatenate(parts[:per]).astype(F32)
-        grad_up = jnp.concatenate(parts[per:2 * per]).astype(F32).T
-        grad_basis = parts[2 * per][:nb].astype(F32)
+        grad_down = reduced[:, :own].astype(F32).reshape(width, feats)
+        grad_up = reduced[:, own:2 * own].astype(F32).reshape(width, feats).T
+        grad_basis = reduced[:-(-nb // (cols - own)), 2 * own:].astype(F32).reshape(-1, feats)[:nb]
         return grad_edges[None], grad_down, grad_up, grad_basis
 
     return shards

time: 231 us -> 227 us (0.983); the launches traced: 230 us -> 224 us
  waiting for transfers between devices: 85.4 us -> 76.4 us
  blocking collectives: 29.4 us -> 32.1 us
    all_to_all x3, waiting for transfers between devices: 74.6 us -> 65.5 us  [exchange(): return lax.all_to_all(x, axes, split_axis=0, concat_axis=0, tiled=True)]
    all_to_all x1 -> x2, blocking collectives: 29.4 us -> 32.1 us  [exchange(): return lax.all_to_all(x, axes, split_axis=0, concat_axis=0, tiled=True)]
  transfers between devices with their start and end apart: 6 -> 6, of which waited for: 6 -> 6; matrix products, arithmetic and copies ran while one was open for 2% -> 2% of each run, Pallas kernels for 10% -> 11%
where the time goes in v6:
time: 227 us; the launch traced here: 224 us
  waiting for transfers between devices  76.4 us (34%)
  Pallas kernels  75.2 us (33%)
  blocking collectives  32.1 us (14%)
  starting transfers between devices  31.8 us (14%)
  local copies, waits for them, and re-layouts  4.12 us (2%)
  other arithmetic  3.32 us (1%)
    all_to_all x3, waiting for transfers between devices, exchange(): return lax.all_to_all(x, axes, split_axis=0, concat_axis=0, tiled=True)  65.5 us
    all_to_all x2, blocking collectives, exchange(): return lax.all_to_all(x, axes, split_axis=0, concat_axis=0, tiled=True)  32.1 us
    all_to_all x3, starting transfers between devices, exchange(): return lax.all_to_all(x, axes, split_axis=0, concat_axis=0, tiled=True)  24.3 us
    pallas_call x1, Pallas kernels, sort_kernel(): pl.pallas_call(body, out_shape=(jax.ShapeDtypeStruct((chunks, rows, LO),...  13.7 us
    pallas_call x1, Pallas kernels, backward_kernel(): pl.pallas_call(body, out_shape=(jax.ShapeDtypeStruct((peers, feats, LO),...  12.4 us
    ppermute x3, waiting for transfers between devices, scatter_dp(): lax.ppermute(give, 'dp', [(k, k ^ 1 << bit) for k in range(n_dp)])  10.9 us
    pallas_call x1, Pallas kernels, forward_kernel(): pl.pallas_call(body, out_shape=(jax.ShapeDtypeStruct((chunks, feats, LO),...  10.5 us
    pallas_call x1, Pallas kernels, send_kernel(): pl.pallas_call(body, out_shape=jax.ShapeDtypeStruct((peers, feats, slot),...  9.03 us
  transfers between devices with their start and end apart: 6, of which 6 were waited for; matrix products, arithmetic and copies ran while one was open for 2% of the time, Pallas kernels for 11%

profile of v6, /device:TPU:1, one launch (start us, length us, event | category | flops | bytes accessed | tf_op | source)
XLA Modules:
  0.0 223.7 jit_solution(2286532571215540276)
XLA Ops:
  0.6 9.0 %send.1 = bf16[32,128,256]{2,1,0:T(8,128)(2,1)} custom-call(bf16[2048,1024]{1,0:T(8,128)(2,1)} %bitcast.20, bf16[1024,128]{1,0:T(8,128)(2,1)} %w_ref.2, s32[1,8192]{1,0:T(1,128)} %i_ref.3), custom_call_target="tpu_custom_call" | custom-call | tf_op jit(solution)/shard_map/send/pallas_call | solution.py:76
  9.7 12.3 %all-to-all-start = ((bf16[32,128,256]{2,1,0:T(8,128)(2,1)}), bf16[32,128,256]{2,1,0:T(8,128)(2,1)S(1)}, u32[]{:S(2)}, u32[]{:S(2)}) async-start(bf16[32,128,256]{2,1,0:T(8,128)(2,1)} %send.1), calls=%async_computation | async-start | bytes 4194304 | tf_op jit(solution)/shard_map/all_to_all | solution.py:516
  22.8 13.7 %order.1 = (f32[32,48,256]{2,1,0:T(8,128)}, s32[2,128]{1,0:T(2,128)}) custom-call(s32[1,8192]{1,0:T(1,128)} %s_ref, s32[1,8192]{1,0:T(1,128)} %d_ref.1, bf16[42,8192]{1,0:T(8,128)(2,1)} %bitcast.25), custom_call_target="tpu_custom_call" | custom-call | tf_op jit(solution)/shard_map/order/pallas_call | solution.py:150
  36.5 34.2 %all-to-all-done.r_ref = bf16[32,128,256]{2,1,0:T(8,128)(2,1)S(1)} async-done(((bf16[32,128,256]{2,1,0:T(8,128)(2,1)}), bf16[32,128,256]{2,1,0:T(8,128)(2,1)S(1)}, u32[]{:S(2)}, u32[]{:S(2)}) %all-to-all-start) | async-done | bytes 2097184 | tf_op jit(solution)/shard_map/all_to_all | solution.py:516
  70.7 10.5 %forward.1 = (bf16[32,128,256]{2,1,0:T(8,128)(2,1)}, bf16[128,2048]{1,0:T(8,128)(2,1)}) custom-call(s32[2,128]{1,0:T(2,128)} %get-tuple-element.18.rg, bf16[32,128,256]{2,1,0:T(8,128)(2,1)S(1)} %all-to-all-done.r_ref, f32[32,48,256]{2,1,0:T(8,128)} %get-tuple-element.19.x_ref, bf16[128,48]{1,0:T(8,128)(2,1)} %pad.8.w_ref), custom_call_target="tpu_custom_call" | custom-call | tf_op jit(solution)/shard_map/forward/pallas_call | solution.py:232
  81.2 7.1 %dense.1 = (bf16[2048,1024]{1,0:T(8,128)(2,1)}, bf16[128,2048]{1,0:T(8,128)(2,1)}) custom-call(bf16[128,2048]{1,0:T(8,128)(2,1)} %get-tuple-element.20.a_ref, bf16[128,1024]{1,0:T(8,128)(2,1)} %w_ref.3, bf16[2048,1024]{1,0:T(8,128)(2,1)} %bitcast.22), custom_call_target="tpu_custom_call" | custom-call | tf_op jit(solution)/shard_map/dense/pallas_call | solution.py:277
  88.3 12.4 %backward.1 = (bf16[32,128,256]{2,1,0:T(8,128)(2,1)}, f32[32,128,256]{2,1,0:T(8,128)}) custom-call(s32[2,128]{1,0:T(2,128)} %get-tuple-element.18.rg, bf16[128,2048]{1,0:T(8,128)(2,1)} %get-tuple-element.21.g_ref, bf16[32,128,256]{2,1,0:T(8,128)(2,1)} %get-tuple-element.22.st_ref, f32[32,48,256]{2,1,0:T(8,128)} %get-tuple-element.19.x_ref, ...), custom_call_target="tpu_custom_call" | custom-call | tf_op jit(solution)/shard_map/backward/pallas_call | solution.py:347
  100.7 7.0 %all-to-all-start.1 = ((bf16[32,128,256]{2,1,0:T(8,128)(2,1)}), bf16[32,128,256]{2,1,0:T(8,128)(2,1)S(1)}, u32[]{:S(2)}, u32[]{:S(2)}) async-start(bf16[32,128,256]{2,1,0:T(8,128)(2,1)} %get-tuple-element.23), calls=%async_computation.1 | async-start | bytes 4194304 | tf_op jit(solution)/shard_map/all_to_all | solution.py:516
  107.7 6.4 %weights.1 = f32[128,1280]{1,0:T(8,128)} custom-call(bf16[128,2048]{1,0:T(8,128)(2,1)} %get-tuple-element.20.a_ref, bf16[2048,1024]{1,0:T(8,128)(2,1)} %get-tuple-element.24.p_ref, f32[32,128,256]{2,1,0:T(8,128)} %get-tuple-element.25.g_ref, f32[32,48,256]{2,1,0:T(8,128)} %get-tuple-element.19.x_ref), custom_call_target="tpu_custom_call" | custom-call | tf_op jit(solution)/shard_map/weights/pallas_call | solution.py:406
  115.2 2.9 %collective-permute-start = (f32[64,1280]{1,0:T(8,128)S(1)}, f32[64,1280]{1,0:T(8,128)S(1)}, u32[]{:S(2)}, u32[]{:S(2)}) collective-permute-start(f32[64,1280]{1,0:T(8,128)S(1)} %constant_dynamic-slice_fusion.2), channel_id=1, source_target_pairs={{0,128},{32,160},{64,192},{96,224},{128,0},{160,32},{192,64},{224,... | collective-permute-start | bytes 983048 | tf_op jit(solution)/shard_map/ppermute | solution.py:557
  118.0 6.7 %collective-permute-done = f32[64,1280]{1,0:T(8,128)S(1)} collective-permute-done((f32[64,1280]{1,0:T(8,128)S(1)}, f32[64,1280]{1,0:T(8,128)S(1)}, u32[]{:S(2)}, u32[]{:S(2)}) %collective-permute-start) | collective-permute-done | bytes 327712 | tf_op jit(solution)/shard_map/ppermute | solution.py:557
  124.7 1.0 dynamic-slice_add_fusion
  125.7 1.5 collective-permute-start.1
  127.3 3.2 %collective-permute-done.1 = f32[32,1280]{1,0:T(8,128)S(1)} collective-permute-done((f32[32,1280]{1,0:T(8,128)S(1)}, f32[32,1280]{1,0:T(8,128)S(1)}, u32[]{:S(2)}, u32[]{:S(2)}) %collective-permute-start.1) | collective-permute-done | bytes 163872 | tf_op jit(solution)/shard_map/ppermute | solution.py:557
  130.6 3.1 %collective-permute-start.2 = (f32[16,1280]{1,0:T(8,128)S(1)}, f32[16,1280]{1,0:T(8,128)S(1)}, u32[]{:S(2)}, u32[]{:S(2)}) collective-permute-start(f32[16,1280]{1,0:T(8,128)S(1)} %constant_dynamic-slice_fusion), channel_id=1, source_target_pairs={{0,32},{32,0},{64,96},{96,64},{128,160},{160,128},{192,224},{224,1... | collective-permute-start | bytes 245768 | tf_op jit(solution)/shard_map/ppermute | solution.py:557
  135.9 20.5 %all-to-all-done.1.r_ref = bf16[32,128,256]{2,1,0:T(8,128)(2,1)S(1)} async-done(((bf16[32,128,256]{2,1,0:T(8,128)(2,1)}), bf16[32,128,256]{2,1,0:T(8,128)(2,1)S(1)}, u32[]{:S(2)}, u32[]{:S(2)}) %all-to-all-start.1) | async-done | bytes 2097184 | tf_op jit(solution)/shard_map/all_to_all | solution.py:516
  156.4 8.7 %returned.1 = (bf16[128,2048]{1,0:T(8,128)(2,1)}, bf16[32,48,128]{2,1,0:T(8,128)(2,1)}) custom-call(bf16[32,128,256]{2,1,0:T(8,128)(2,1)S(1)} %all-to-all-done.1.r_ref, s32[1,8192]{1,0:T(1,128)} %i_ref.3, bf16[2048,1024]{1,0:T(8,128)(2,1)} %bitcast.21, bf16[32,16,128]{2,1,0:T(8,128)(2,1)} %fusion.2.p_ref), custom_call_target="tpu_custom_call" | custom-call | tf_op jit(solution)/shard_map/returned/pallas_call | solution.py:471
  165.1 18.1 %all_to_all.25.x_ref = bf16[32,48,128]{2,1,0:T(8,128)(2,1)} all-to-all(bf16[32,48,128]{2,1,0:T(8,128)(2,1)} %get-tuple-element.29), channel_id=1, replica_groups=mesh['dp'=8,'graph'=32] {'graph'}, dimensions={0} | all-to-all | bytes 786432 | tf_op jit(solution)/shard_map/all_to_all | solution.py:516
  183.2 1.7 graph_sum.1
  184.9 14.0 %all_to_all.26.x_ref = bf16[8,48,128]{2,1,0:T(8,128)(2,1)} all-to-all(bf16[8,48,128]{2,1,0:T(8,128)(2,1)} %graph_sum.1), channel_id=1, replica_groups=mesh['dp'=8,'graph'=32] {'dp'}, dimensions={0} | all-to-all | bytes 196608 | tf_op jit(solution)/shard_map/all_to_all | solution.py:516
  198.9 1.8 dp_sum.1
  200.8 4.9 %all-to-all-start.4 = ((bf16[32,72,128]{2,1,0:T(8,128)(2,1)}), bf16[32,72,128]{2,1,0:T(8,128)(2,1)S(1)}, u32[]{:S(2)}, u32[]{:S(2)}) async-start(bf16[32,72,128]{2,1,0:T(8,128)(2,1)} %dp_sum.1), calls=%async_computation.4 | async-start | bytes 1179648 | tf_op jit(solution)/shard_map/all_to_all | solution.py:516
  206.6 3.8 %grad_edges.1 = bf16[2048,1024]{1,0:T(8,128)(2,1)} custom-call(bf16[128,2048]{1,0:T(8,128)(2,1)} %get-tuple-element.28.g_ref, bf16[128,1024]{1,0:T(8,128)(2,1)} %bitcast.24), custom_call_target="tpu_custom_call" | custom-call | tf_op jit(solution)/shard_map/grad_edges/pallas_call | solution.py:504
  210.4 10.8 %all-to-all-done.4 = bf16[32,72,128]{2,1,0:T(8,128)(2,1)S(1)} async-done(((bf16[32,72,128]{2,1,0:T(8,128)(2,1)}), bf16[32,72,128]{2,1,0:T(8,128)(2,1)S(1)}, u32[]{:S(2)}, u32[]{:S(2)}) %all-to-all-start.4) | async-done | bytes 589856 | tf_op jit(solution)/shard_map/all_to_all | solution.py:516
  (25 shorter events, 7.4 us)
Async XLA Ops:
  9.7 12.3 %copy-start.1 = (bf16[42,128]{1,0:T(8,128)(2,1)S(1)}, bf16[42,128]{1,0:T(8,128)(2,1)}, u32[]{:S(2)}) copy-start(bf16[42,128]{1,0:T(8,128)(2,1)} %param.17) | copy-start | bytes 32260
  9.7 61.0 %all-to-all-start = ((bf16[32,128,256]{2,1,0:T(8,128)(2,1)}), bf16[32,128,256]{2,1,0:T(8,128)(2,1)S(1)}, u32[]{:S(2)}, u32[]{:S(2)}) async-start(bf16[32,128,256]{2,1,0:T(8,128)(2,1)} %send.1), calls=%async_computation | async-start | bytes 4194304 | tf_op jit(solution)/shard_map/all_to_all | solution.py:516
  100.7 55.7 %all-to-all-start.1 = ((bf16[32,128,256]{2,1,0:T(8,128)(2,1)}), bf16[32,128,256]{2,1,0:T(8,128)(2,1)S(1)}, u32[]{:S(2)}, u32[]{:S(2)}) async-start(bf16[32,128,256]{2,1,0:T(8,128)(2,1)} %get-tuple-element.23), calls=%async_computation.1 | async-start | bytes 4194304 | tf_op jit(solution)/shard_map/all_to_all | solution.py:516
  115.2 9.6 %collective-permute-start = (f32[64,1280]{1,0:T(8,128)S(1)}, f32[64,1280]{1,0:T(8,128)S(1)}, u32[]{:S(2)}, u32[]{:S(2)}) collective-permute-start(f32[64,1280]{1,0:T(8,128)S(1)} %constant_dynamic-slice_fusion.2), channel_id=1, source_target_pairs={{0,128},{32,160},{64,192},{96,224},{128,0},{160,32},{192,64},{224,... | collective-permute-start | bytes 983048 | tf_op jit(solution)/shard_map/ppermute | solution.py:557
  125.7 4.8 %collective-permute-start.1 = (f32[32,1280]{1,0:T(8,128)S(1)}, f32[32,1280]{1,0:T(8,128)S(1)}, u32[]{:S(2)}, u32[]{:S(2)}) collective-permute-start(f32[32,1280]{1,0:T(8,128)S(1)} %constant_dynamic-slice_fusion.1), channel_id=1, source_target_pairs={{0,64},{32,96},{64,0},{96,32},{128,192},{160,224},{192,128},{224,1... | collective-permute-start | bytes 491528 | tf_op jit(solution)/shard_map/ppermute | solution.py:557
  130.6 4.0 %collective-permute-start.2 = (f32[16,1280]{1,0:T(8,128)S(1)}, f32[16,1280]{1,0:T(8,128)S(1)}, u32[]{:S(2)}, u32[]{:S(2)}) collective-permute-start(f32[16,1280]{1,0:T(8,128)S(1)} %constant_dynamic-slice_fusion), channel_id=1, source_target_pairs={{0,32},{32,0},{64,96},{96,64},{128,160},{160,128},{192,224},{224,1... | collective-permute-start | bytes 245768 | tf_op jit(solution)/shard_map/ppermute | solution.py:557
  165.1 40.6 %copy-start = (bf16[1024,128]{1,0:T(8,128)(2,1)S(1)}, bf16[1024,128]{1,0:T(8,128)(2,1)}, u32[]{:S(2)}) copy-start(bf16[1024,128]{1,0:T(8,128)(2,1)} %w_ref.2) | copy-start | bytes 786436
  200.8 20.4 %all-to-all-start.4 = ((bf16[32,72,128]{2,1,0:T(8,128)(2,1)}), bf16[32,72,128]{2,1,0:T(8,128)(2,1)S(1)}, u32[]{:S(2)}, u32[]{:S(2)}) async-start(bf16[32,72,128]{2,1,0:T(8,128)(2,1)} %dp_sum.1), calls=%async_computation.4 | async-start | bytes 1179648 | tf_op jit(solution)/shard_map/all_to_all | solution.py:516

commit v7 on v6

--- a/solution.py
+++ b/solution.py
@@ -39,7 +39,7 @@
 
 
 def params():
-    return pltpu.CompilerParams(vmem_limit_bytes=56 * 1024 * 1024)
+    return pltpu.CompilerParams(vmem_limit_bytes=48 * 1024 * 1024)
 
 
 def full(shape):

time: 227 us -> 227 us (level)
  Pallas kernels: 75.2 us -> 65.8 us
  waiting for transfers between devices: 76.4 us -> 84.7 us
  local copies, waits for them, and re-layouts: 4.12 us -> 6.9 us
    all_to_all x3, waiting for transfers between devices: 65.5 us -> 73.6 us  [exchange(): return lax.all_to_all(x, axes, split_axis=0, concat_axis=0, tiled=True)]
    unnamed x6 -> x24, local copies, waits for them, and re-layouts: 0.98 us -> 5.33 us
  transfers between devices with their start and end apart: 6 -> 6, of which waited for: 6 -> 6; matrix products, arithmetic and copies ran while one was open for 2% -> 0% of each run, Pallas kernels for 11% -> 9%
where the time goes in v7:
time: 227 us; the launch traced here: 223 us
  waiting for transfers between devices  84.7 us (37%)
  Pallas kernels  65.8 us (29%)
  starting transfers between devices  31.8 us (14%)
  blocking collectives  31.5 us (14%)
  local copies, waits for them, and re-layouts  6.9 us (3%)
    all_to_all x3, waiting for transfers between devices, exchange(): return lax.all_to_all(x, axes, split_axis=0, concat_axis=0, tiled=True)  73.6 us
    all_to_all x2, blocking collectives, exchange(): return lax.all_to_all(x, axes, split_axis=0, concat_axis=0, tiled=True)  31.5 us
    all_to_all x3, starting transfers between devices, exchange(): return lax.all_to_all(x, axes, split_axis=0, concat_axis=0, tiled=True)  24.5 us
    pallas_call x1, Pallas kernels, sort_kernel(): pl.pallas_call(body, out_shape=(jax.ShapeDtypeStruct((chunks, rows, LO),...  11.6 us
    pallas_call x1, Pallas kernels, backward_kernel(): pl.pallas_call(body, out_shape=(jax.ShapeDtypeStruct((peers, feats, LO),...  11.2 us
    ppermute x3, waiting for transfers between devices, scatter_dp(): lax.ppermute(give, 'dp', [(k, k ^ 1 << bit) for k in range(n_dp)])  11.1 us
    pallas_call x1, Pallas kernels, forward_kernel(): pl.pallas_call(body, out_shape=(jax.ShapeDtypeStruct((chunks, feats, LO),...  10.7 us
    pallas_call x1, Pallas kernels, send_kernel(): pl.pallas_call(body, out_shape=jax.ShapeDtypeStruct((peers, feats, slot),...  8.96 us
  transfers between devices with their start and end apart: 6, of which 6 were waited for; matrix products, arithmetic and copies ran while one was open for 0% of the time, Pallas kernels for 9%

profile of v7, /device:TPU:1, one launch (start us, length us, event | category | flops | bytes accessed | tf_op | source)
XLA Modules:
  0.0 223.3 jit_solution(3734520065342955818)
XLA Ops:
  2.3 9.0 %send.1 = bf16[32,128,256]{2,1,0:T(8,128)(2,1)} custom-call(bf16[2048,1024]{1,0:T(8,128)(2,1)} %bitcast.22, bf16[1024,128]{1,0:T(8,128)(2,1)S(1)} %copy-done.2, s32[1,8192]{1,0:T(1,128)S(1)} %copy-done.6), custom_call_target="tpu_custom_call" | custom-call | tf_op jit(solution)/shard_map/send/pallas_call | solution.py:76
  11.3 12.5 %all-to-all-start = ((bf16[32,128,256]{2,1,0:T(8,128)(2,1)}), bf16[32,128,256]{2,1,0:T(8,128)(2,1)}, u32[]{:S(2)}, u32[]{:S(2)}) async-start(bf16[32,128,256]{2,1,0:T(8,128)(2,1)} %send.1), calls=%async_computation | async-start | bytes 4194304 | tf_op jit(solution)/shard_map/all_to_all | solution.py:516
  24.0 11.6 %order.1 = (f32[32,48,256]{2,1,0:T(8,128)S(1)}, s32[2,128]{1,0:T(2,128)S(1)}) custom-call(s32[1,8192]{1,0:T(1,128)S(1)} %copy-done.8, s32[1,8192]{1,0:T(1,128)S(1)} %copy-done.9, bf16[42,8192]{1,0:T(8,128)(2,1)S(1)} %bitcast.21), custom_call_target="tpu_custom_call" | custom-call | tf_op jit(solution)/shard_map/order/pallas_call | solution.py:150
  35.6 36.9 %all-to-all-done.r_ref = bf16[32,128,256]{2,1,0:T(8,128)(2,1)} async-done(((bf16[32,128,256]{2,1,0:T(8,128)(2,1)}), bf16[32,128,256]{2,1,0:T(8,128)(2,1)}, u32[]{:S(2)}, u32[]{:S(2)}) %all-to-all-start) | async-done | bytes 2097184 | tf_op jit(solution)/shard_map/all_to_all | solution.py:516
  72.5 10.7 %forward.1 = (bf16[32,128,256]{2,1,0:T(8,128)(2,1)}, bf16[128,2048]{1,0:T(8,128)(2,1)S(1)}) custom-call(s32[2,128]{1,0:T(2,128)S(1)} %get-tuple-element.18.rg, bf16[32,128,256]{2,1,0:T(8,128)(2,1)} %all-to-all-done.r_ref, f32[32,48,256]{2,1,0:T(8,128)S(1)} %get-tuple-element.19.x_ref, bf16[128,48]{1,0:T(8,128)(2,1)S(1)} %pad.8.w_ref), custom_call_target="tpu_custom_call" | custom-call | tf_op jit(solution)/shard_map/forward/pallas_call | solution.py:232
  83.2 5.8 %dense.1 = (bf16[2048,1024]{1,0:T(8,128)(2,1)S(1)}, bf16[128,2048]{1,0:T(8,128)(2,1)S(1)}) custom-call(bf16[128,2048]{1,0:T(8,128)(2,1)S(1)} %get-tuple-element.20.a_ref, bf16[128,1024]{1,0:T(8,128)(2,1)S(1)} %copy-done.5, bf16[2048,1024]{1,0:T(8,128)(2,1)} %bitcast.24), custom_call_target="tpu_custom_call" | custom-call | tf_op jit(solution)/shard_map/dense/pallas_call | solution.py:277
  89.0 1.9 copy-done
  90.9 11.2 %backward.1 = (bf16[32,128,256]{2,1,0:T(8,128)(2,1)S(1)}, f32[32,128,256]{2,1,0:T(8,128)}) custom-call(s32[2,128]{1,0:T(2,128)S(1)} %get-tuple-element.18.rg, bf16[128,2048]{1,0:T(8,128)(2,1)S(1)} %get-tuple-element.21.g_ref, bf16[32,128,256]{2,1,0:T(8,128)(2,1)} %get-tuple-element.22.st_ref, f32[32,48,256]{2,1,0:T(8,128)S(1)} %get-tuple-element.19.x_ref, ...), custom_call_target="tpu_custom_call" | custom-call | tf_op jit(solution)/shard_map/backward/pallas_call | solution.py:347
  102.1 1.4 copy-done.1
  103.5 7.1 %all-to-all-start.1 = ((bf16[32,128,256]{2,1,0:T(8,128)(2,1)}), bf16[32,128,256]{2,1,0:T(8,128)(2,1)}, u32[]{:S(2)}, u32[]{:S(2)}) async-start(bf16[32,128,256]{2,1,0:T(8,128)(2,1)} %copy-done.1), calls=%async_computation.1 | async-start | bytes 4194304 | tf_op jit(solution)/shard_map/all_to_all | solution.py:516
  110.6 5.2 %weights.1 = f32[128,1280]{1,0:T(8,128)S(1)} custom-call(bf16[128,2048]{1,0:T(8,128)(2,1)S(1)} %get-tuple-element.20.a_ref, bf16[2048,1024]{1,0:T(8,128)(2,1)} %copy-done, f32[32,128,256]{2,1,0:T(8,128)} %get-tuple-element.25.g_ref, f32[32,48,256]{2,1,0:T(8,128)S(1)} %get-tuple-element.19.x_ref), custom_call_target="tpu_custom_call" | custom-call | tf_op jit(solution)/shard_map/weights/pallas_call | solution.py:406
  115.9 3.1 %collective-permute-start = (f32[64,1280]{1,0:T(8,128)S(1)}, f32[64,1280]{1,0:T(8,128)S(1)}, u32[]{:S(2)}, u32[]{:S(2)}) collective-permute-start(f32[64,1280]{1,0:T(8,128)S(1)} %constant_dynamic-slice_fusion.2), channel_id=1, source_target_pairs={{0,128},{32,160},{64,192},{96,224},{128,0},{160,32},{192,64},{224,... | collective-permute-start | bytes 983048 | tf_op jit(solution)/shard_map/ppermute | solution.py:557
  118.9 6.8 %collective-permute-done = f32[64,1280]{1,0:T(8,128)S(1)} collective-permute-done((f32[64,1280]{1,0:T(8,128)S(1)}, f32[64,1280]{1,0:T(8,128)S(1)}, u32[]{:S(2)}, u32[]{:S(2)}) %collective-permute-start) | collective-permute-done | bytes 327712 | tf_op jit(solution)/shard_map/ppermute | solution.py:557
  125.8 1.3 collective-permute-start.1
  127.1 3.4 %collective-permute-done.1 = f32[32,1280]{1,0:T(8,128)S(1)} collective-permute-done((f32[32,1280]{1,0:T(8,128)S(1)}, f32[32,1280]{1,0:T(8,128)S(1)}, u32[]{:S(2)}, u32[]{:S(2)}) %collective-permute-start.1) | collective-permute-done | bytes 163872 | tf_op jit(solution)/shard_map/ppermute | solution.py:557
  130.5 2.9 %collective-permute-start.2 = (f32[16,1280]{1,0:T(8,128)S(1)}, f32[16,1280]{1,0:T(8,128)S(1)}, u32[]{:S(2)}, u32[]{:S(2)}) collective-permute-start(f32[16,1280]{1,0:T(8,128)S(1)} %constant_dynamic-slice_fusion), channel_id=1, source_target_pairs={{0,32},{32,0},{64,96},{96,64},{128,160},{160,128},{192,224},{224,1... | collective-permute-start | bytes 245768 | tf_op jit(solution)/shard_map/ppermute | solution.py:557
  135.0 24.3 %all-to-all-done.1.r_ref = bf16[32,128,256]{2,1,0:T(8,128)(2,1)} async-done(((bf16[32,128,256]{2,1,0:T(8,128)(2,1)}), bf16[32,128,256]{2,1,0:T(8,128)(2,1)}, u32[]{:S(2)}, u32[]{:S(2)}) %all-to-all-start.1) | async-done | bytes 2097184 | tf_op jit(solution)/shard_map/all_to_all | solution.py:516
  159.3 8.5 %returned.1 = (bf16[128,2048]{1,0:T(8,128)(2,1)S(1)}, bf16[32,48,128]{2,1,0:T(8,128)(2,1)S(1)}) custom-call(bf16[32,128,256]{2,1,0:T(8,128)(2,1)} %all-to-all-done.1.r_ref, s32[1,8192]{1,0:T(1,128)S(1)} %copy-done.7, bf16[2048,1024]{1,0:T(8,128)(2,1)} %bitcast.23, bf16[32,16,128]{2,1,0:T(8,128)(2,1)S(1)} %fusion.2.p_ref), custom_call_target="tpu_custom_call" | custom-call | tf_op jit(solution)/shard_map/returned/pallas_call | solution.py:471
  167.8 17.8 %all_to_all.25.x_ref = bf16[32,48,128]{2,1,0:T(8,128)(2,1)S(1)} all-to-all(bf16[32,48,128]{2,1,0:T(8,128)(2,1)S(1)} %get-tuple-element.29), channel_id=1, replica_groups=mesh['dp'=8,'graph'=32] {'graph'}, dimensions={0} | all-to-all | bytes 786432 | tf_op jit(solution)/shard_map/all_to_all | solution.py:516
  185.7 13.7 %all_to_all.26.x_ref = bf16[8,48,128]{2,1,0:T(8,128)(2,1)S(1)} all-to-all(bf16[8,48,128]{2,1,0:T(8,128)(2,1)S(1)} %graph_sum.1), channel_id=1, replica_groups=mesh['dp'=8,'graph'=32] {'dp'}, dimensions={0} | all-to-all | bytes 196608 | tf_op jit(solution)/shard_map/all_to_all | solution.py:516
  200.3 4.9 %all-to-all-start.4 = ((bf16[32,72,128]{2,1,0:T(8,128)(2,1)}), bf16[32,72,128]{2,1,0:T(8,128)(2,1)S(1)}, u32[]{:S(2)}, u32[]{:S(2)}) async-start(bf16[32,72,128]{2,1,0:T(8,128)(2,1)} %dp_sum.1), calls=%async_computation.4 | async-start | bytes 1179648 | tf_op jit(solution)/shard_map/all_to_all | solution.py:516
  205.4 2.9 %grad_edges.1 = bf16[2048,1024]{1,0:T(8,128)(2,1)} custom-call(bf16[128,2048]{1,0:T(8,128)(2,1)S(1)} %get-tuple-element.28.g_ref, bf16[128,1024]{1,0:T(8,128)(2,1)S(1)} %bitcast.20), custom_call_target="tpu_custom_call" | custom-call | tf_op jit(solution)/shard_map/grad_edges/pallas_call | solution.py:504
  208.3 12.4 %all-to-all-done.4 = bf16[32,72,128]{2,1,0:T(8,128)(2,1)S(1)} async-done(((bf16[32,72,128]{2,1,0:T(8,128)(2,1)}), bf16[32,72,128]{2,1,0:T(8,128)(2,1)S(1)}, u32[]{:S(2)}, u32[]{:S(2)}) %all-to-all-start.4) | async-done | bytes 589856 | tf_op jit(solution)/shard_map/all_to_all | solution.py:516
  221.6 1.0 copy.21
  (43 shorter events, 6.2 us)
Async XLA Ops:
  0.6 1.0 copy-start.2
  1.6 0.8 copy-start.6
  11.3 12.5 %copy-start.10 = (bf16[42,128]{1,0:T(8,128)(2,1)S(1)}, bf16[42,128]{1,0:T(8,128)(2,1)}, u32[]{:S(2)}) copy-start(bf16[42,128]{1,0:T(8,128)(2,1)} %param.17) | copy-start | bytes 32260
  11.3 12.7 %copy-start.4 = (bf16[1,42,8192]{2,1,0:T(8,128)(2,1)S(1)}, bf16[1,42,8192]{2,1,0:T(8,128)(2,1)}, u32[]{:S(2)}) copy-start(bf16[1,42,8192]{2,1,0:T(8,128)(2,1)} %param.13) | copy-start | bytes 2064388
  11.3 12.7 %copy-start.8 = (s32[1,8192]{1,0:T(1,128)S(1)}, s32[1,8192]{1,0:T(1,128)}, u32[]{:S(2)}) copy-start(s32[1,8192]{1,0:T(1,128)} %s_ref) | copy-start | bytes 98308
  11.3 12.7 %copy-start.9 = (s32[1,8192]{1,0:T(1,128)S(1)}, s32[1,8192]{1,0:T(1,128)}, u32[]{:S(2)}) copy-start(s32[1,8192]{1,0:T(1,128)} %d_ref.1) | copy-start | bytes 98308
  11.3 61.2 %all-to-all-start = ((bf16[32,128,256]{2,1,0:T(8,128)(2,1)}), bf16[32,128,256]{2,1,0:T(8,128)(2,1)}, u32[]{:S(2)}, u32[]{:S(2)}) async-start(bf16[32,128,256]{2,1,0:T(8,128)(2,1)} %send.1), calls=%async_computation | async-start | bytes 4194304 | tf_op jit(solution)/shard_map/all_to_all | solution.py:516
  24.0 59.2 %copy-start.5 = (bf16[128,1024]{1,0:T(8,128)(2,1)S(1)}, bf16[128,1024]{1,0:T(8,128)(2,1)}, u32[]{:S(2)}) copy-start(bf16[128,1024]{1,0:T(8,128)(2,1)} %w_ref.3) | copy-start | bytes 786436
  89.0 1.9 copy-start
  102.1 1.4 copy-start.1
  103.5 55.8 %all-to-all-start.1 = ((bf16[32,128,256]{2,1,0:T(8,128)(2,1)}), bf16[32,128,256]{2,1,0:T(8,128)(2,1)}, u32[]{:S(2)}, u32[]{:S(2)}) async-start(bf16[32,128,256]{2,1,0:T(8,128)(2,1)} %copy-done.1), calls=%async_computation.1 | async-start | bytes 4194304 | tf_op jit(solution)/shard_map/all_to_all | solution.py:516
  115.8 43.4 %copy-start.7 = (s32[1,8192]{1,0:T(1,128)S(1)}, s32[1,8192]{1,0:T(1,128)}, u32[]{:S(2)}) copy-start(s32[1,8192]{1,0:T(1,128)} %i_ref.3) | copy-start | bytes 98308
  115.9 9.9 %collective-permute-start = (f32[64,1280]{1,0:T(8,128)S(1)}, f32[64,1280]{1,0:T(8,128)S(1)}, u32[]{:S(2)}, u32[]{:S(2)}) collective-permute-start(f32[64,1280]{1,0:T(8,128)S(1)} %constant_dynamic-slice_fusion.2), channel_id=1, source_target_pairs={{0,128},{32,160},{64,192},{96,224},{128,0},{160,32},{192,64},{224,... | collective-permute-start | bytes 983048 | tf_op jit(solution)/shard_map/ppermute | solution.py:557
  125.8 4.7 %collective-permute-start.1 = (f32[32,1280]{1,0:T(8,128)S(1)}, f32[32,1280]{1,0:T(8,128)S(1)}, u32[]{:S(2)}, u32[]{:S(2)}) collective-permute-start(f32[32,1280]{1,0:T(8,128)S(1)} %constant_dynamic-slice_fusion.1), channel_id=1, source_target_pairs={{0,64},{32,96},{64,0},{96,32},{128,192},{160,224},{192,128},{224,1... | collective-permute-start | bytes 491528 | tf_op jit(solution)/shard_map/ppermute | solution.py:557
  130.5 3.8 %collective-permute-start.2 = (f32[16,1280]{1,0:T(8,128)S(1)}, f32[16,1280]{1,0:T(8,128)S(1)}, u32[]{:S(2)}, u32[]{:S(2)}) collective-permute-start(f32[16,1280]{1,0:T(8,128)S(1)} %constant_dynamic-slice_fusion), channel_id=1, source_target_pairs={{0,32},{32,0},{64,96},{96,64},{128,160},{160,128},{192,224},{224,1... | collective-permute-start | bytes 245768 | tf_op jit(solution)/shard_map/ppermute | solution.py:557
  167.7 37.5 %copy-start.3 = (bf16[1024,128]{1,0:T(8,128)(2,1)S(1)}, bf16[1024,128]{1,0:T(8,128)(2,1)}, u32[]{:S(2)}) copy-start(bf16[1024,128]{1,0:T(8,128)(2,1)} %w_ref.2) | copy-start | bytes 786436
  200.3 20.4 %all-to-all-start.4 = ((bf16[32,72,128]{2,1,0:T(8,128)(2,1)}), bf16[32,72,128]{2,1,0:T(8,128)(2,1)S(1)}, u32[]{:S(2)}, u32[]{:S(2)}) async-start(bf16[32,72,128]{2,1,0:T(8,128)(2,1)} %dp_sum.1), calls=%async_computation.4 | async-start | bytes 1179648 | tf_op jit(solution)/shard_map/all_to_all | solution.py:516
